TPU v7x, 32 devices: a whole 2x2x4 slice. The times are simulated.
32 devices in a mesh: seq: 4 (over y, x), batch: 8 (over z, core).
Axes of the slice: x: 2, y: 2, z: 4, core: 2. Of those that a mesh axis runs over, the one named last changes fastest.
Arguments:
- tokens: bfloat16 [8, 1024, 2048], P('batch', 'seq'), may hold values from -48 to 48
- seq_count: int32 [8], P('batch'), may hold values from 1 to 4, as said below
- query_weight: bfloat16 [2048, 2048], P(None, 'seq'), may hold values from -0.125 to 0.125
- key_weight: bfloat16 [2048, 256], P(None, 'seq'), may hold values from -0.125 to 0.125
- value_weight: bfloat16 [2048, 256], P(None, 'seq'), may hold values from -0.125 to 0.125
- out_weight: bfloat16 [2048, 2048], P('seq'), may hold values from -0.5 to 0.5
- gate_weight: bfloat16 [2048, 5632], P(None, 'seq'), may hold values from -0.125 to 0.125
- up_weight: bfloat16 [2048, 5632], P(None, 'seq'), may hold values from -0.125 to 0.125
- down_weight: bfloat16 [5632, 2048], P('seq'), may hold values from -0.078125 to 0.078125
- attention_gain: float32 [2048], replicated, may hold values from 0.5 to 1.5
- feedforward_gain: float32 [2048], replicated, may hold values from 0.5 to 1.5
- cotangent: bfloat16 [8, 1024, 2048], P('batch', 'seq'), may hold values from -6 to 6
Outputs:
- layer_out: bfloat16 [8, 1024, 2048], P('batch', 'seq')
- input_grad: float32 [8, 1024, 2048], P('batch', 'seq')
- query_grad: float32 [2048, 2048], P('batch', 'seq')
- key_grad: float32 [2048, 256], P('batch', 'seq')
- value_grad: float32 [2048, 256], P('batch', 'seq')
- out_grad: float32 [2048, 2048], P(('seq', 'batch'))
- gate_grad: float32 [2048, 5632], P('batch', 'seq')
- up_grad: float32 [2048, 5632], P('batch', 'seq')
- down_grad: float32 [5632, 2048], P(('seq', 'batch'))
- attention_gain_grad: float32 [2048], P(('seq', 'batch'))
- feedforward_gain_grad: float32 [2048], P(('seq', 'batch'))
Inputs may be any that keep to these rules, and one draw needn't show every extreme that they name: `seq_count`: the 1024 tokens of a group form this many sequences of equal length, one after another; the values are 1, 2 and 4, and each of them occurs in some group.
All inputs are finite; a program needn't handle non-finite values.
Results may differ from a plain program's by a relative error of at most 0.02.
Values may be sent and summed in bfloat16 or wider, within the bound.
No kernel may reach another device: no remote copies, remote signals or barrier semaphores. Data moves between devices by JAX's collectives and lax.ppermute only.
A program may use at most 192 MiB of HBM per device.

v0:
```python
import math

import jax
import jax.numpy as jnp
from jax import lax
from jax.sharding import PartitionSpec as P

H = 32
KVH = 4
HD = 64


EPS = 1e-05
NEG = -1e30


def rotation(positions):
    freq_index = jnp.arange(HD // 2, dtype=jnp.float32)
    inverse = jnp.exp(freq_index * (-2.0 * math.log(10000.0) / HD))
    angles = positions.astype(jnp.float32)[:, None] * inverse[None, :]
    return (jnp.cos(angles)[:, None, :], jnp.sin(angles)[:, None, :])


def rotate(values, cosine_table, sine_table):
    half_width = HD // 2
    first_half = values[..., :half_width]
    second_half = values[..., half_width:]
    return jnp.concatenate(
        [
            first_half * cosine_table - second_half * sine_table,
            second_half * cosine_table + first_half * sine_table,
        ],
        axis=-1,
    )


def rotate_back(grads, cosine_table, sine_table):
    half_width = HD // 2
    first_half = grads[..., :half_width]
    second_half = grads[..., half_width:]
    return jnp.concatenate(
        [
            first_half * cosine_table + second_half * sine_table,
            second_half * cosine_table - first_half * sine_table,
        ],
        axis=-1,
    )


def norm_forward(values, gain):
    norm_scale = lax.rsqrt(jnp.mean(values * values, axis=-1, keepdims=True) + EPS)
    return (values * norm_scale * gain, norm_scale)


def norm_backward(values, norm_scale, gain, grads):
    weighted = grads * gain
    gain_grad = jnp.sum(grads * values * norm_scale, axis=0)
    cubed = norm_scale * norm_scale * norm_scale
    value_grad = norm_scale * weighted - values * cubed * jnp.mean(
        weighted * values, axis=-1, keepdims=True
    )
    return (gain_grad, value_grad)


def masked_scores(query_block, key_part, query_starts, row_first, key_first):
    block_rows = query_block.shape[0]
    query_index = row_first + jnp.arange(block_rows, dtype=jnp.int32)
    key_index = key_first + jnp.arange(key_part.shape[0], dtype=jnp.int32)
    allowed = (key_index[None, :] <= query_index[:, None]) & (
        key_index[None, :] >= query_starts[:, None]
    )
    scores = jnp.einsum(
        "qngd,knd->ngqk", query_block, key_part, preferred_element_type=jnp.float32
    ) * (1.0 / math.sqrt(HD))
    return jnp.where(allowed, scores, NEG)


def block_forward(query_block, key_heads, value_heads, query_starts, row_first, key_first):
    row_last = row_first + query_block.shape[0]
    scores = masked_scores(
        query_block, key_heads[key_first:row_last], query_starts, row_first, key_first
    )
    row_max = jnp.max(scores, axis=-1, keepdims=True)
    exponent = jnp.exp(scores - row_max)
    exp_total = jnp.sum(exponent, axis=-1, keepdims=True)
    soft_probs = (exponent / exp_total).astype(jnp.bfloat16)
    result = jnp.einsum(
        "ngqk,knd->qngd",
        soft_probs,
        value_heads[key_first:row_last],
        preferred_element_type=jnp.float32,
    )
    return (result, row_max + jnp.log(exp_total))


def block_backward(
    query_block, key_heads, value_heads, grad_block, lse_block, query_starts, row_first, key_first
):
    row_last = row_first + query_block.shape[0]
    key_part = key_heads[key_first:row_last]
    value_part = value_heads[key_first:row_last]
    scores = masked_scores(query_block, key_part, query_starts, row_first, key_first)
    soft_probs = jnp.exp(scores - lse_block)
    grad_probs = jnp.einsum(
        "qngd,knd->ngqk", grad_block, value_part, preferred_element_type=jnp.float32
    )
    row_delta = jnp.sum(soft_probs * grad_probs, axis=-1, keepdims=True)
    grad_scores = (soft_probs * (grad_probs - row_delta)).astype(jnp.bfloat16)
    score_scale = 1.0 / math.sqrt(HD)
    grad_query = (
        jnp.einsum("ngqk,knd->qngd", grad_scores, key_part, preferred_element_type=jnp.float32)
        * score_scale
    )
    grad_key = (
        jnp.einsum("ngqk,qngd->knd", grad_scores, query_block, preferred_element_type=jnp.float32)
        * score_scale
    )
    grad_value = jnp.einsum(
        "ngqk,qngd->knd",
        soft_probs.astype(jnp.bfloat16),
        grad_block,
        preferred_element_type=jnp.float32,
    )
    padding = ((key_first, key_heads.shape[0] - row_last), (0, 0), (0, 0))
    return (grad_query, jnp.pad(grad_key, padding), jnp.pad(grad_value, padding))


def shards(
    tokens,
    seq_count,
    query_weight,
    key_weight,
    value_weight,
    out_weight,
    gate_weight,
    up_weight,
    down_weight,
    attention_gain,
    feedforward_gain,
    cotangent,
):
    seq_parts = lax.axis_size("seq")
    local_rows = tokens.shape[1]
    model_width = tokens.shape[2]
    group_rows = local_rows * seq_parts
    block_rows = min(512, group_rows)
    heads_local = query_weight.shape[1] // HD
    kv_local = key_weight.shape[1] // HD
    head_share = H // KVH
    seq_length = group_rows // seq_count[0]
    group_index = jnp.arange(group_rows, dtype=jnp.int32)
    starts = group_index // seq_length * seq_length
    cosine_table, sine_table = rotation(group_index - starts)
    inputs = tokens[0].astype(jnp.float32)
    normed_value, scale_one = norm_forward(inputs, attention_gain)
    normed_one = normed_value.astype(jnp.bfloat16)
    normed_rows = lax.all_gather(normed_one, "seq", axis=0, tiled=True)
    query_pre = jnp.dot(normed_rows, query_weight, preferred_element_type=jnp.float32)
    key_pre = jnp.dot(normed_rows, key_weight, preferred_element_type=jnp.float32)
    value_heads = (
        jnp.dot(normed_rows, value_weight, preferred_element_type=jnp.float32)
        .astype(jnp.bfloat16)
        .reshape(group_rows, kv_local, HD)
    )
    query_heads = (
        rotate(query_pre.reshape(group_rows, heads_local, HD), cosine_table, sine_table)
        .astype(jnp.bfloat16)
        .reshape(group_rows, kv_local, head_share, HD)
    )
    key_heads = rotate(key_pre.reshape(group_rows, kv_local, HD), cosine_table, sine_table).astype(
        jnp.bfloat16
    )
    head_outputs = []
    lse_blocks = []
    for block_index in range(group_rows // block_rows):
        row_first = block_index * block_rows
        row_last = row_first + block_rows
        query_block = query_heads[row_first:row_last]
        query_starts = starts[row_first:row_last]
        block_out, block_lse = block_forward(
            query_block, key_heads, value_heads, query_starts, row_first, 0
        )
        head_outputs.append(block_out)
        lse_blocks.append(block_lse)
    attended = (
        jnp.concatenate(head_outputs, axis=0)
        .astype(jnp.bfloat16)
        .reshape(group_rows, heads_local * HD)
    )
    branch = lax.psum_scatter(
        jnp.dot(attended, out_weight, preferred_element_type=jnp.float32),
        "seq",
        scatter_dimension=0,
        tiled=True,
    )
    hidden = inputs + branch
    normed_mid, scale_two = norm_forward(hidden, feedforward_gain)
    normed_two = normed_mid.astype(jnp.bfloat16)
    normed_two_rows = lax.all_gather(normed_two, "seq", axis=0, tiled=True)
    gate = jnp.dot(normed_two_rows, gate_weight, preferred_element_type=jnp.float32)
    upward = jnp.dot(normed_two_rows, up_weight, preferred_element_type=jnp.float32)
    sigmoid_gate = jax.nn.sigmoid(gate)
    activated = gate * sigmoid_gate
    mixed = (activated * upward).astype(jnp.bfloat16)
    ffn_out = lax.psum_scatter(
        jnp.dot(mixed, down_weight, preferred_element_type=jnp.float32).astype(jnp.bfloat16),
        "seq",
        scatter_dimension=0,
        tiled=True,
    ).astype(jnp.float32)
    layer_out = (hidden + ffn_out).astype(jnp.bfloat16)
    grad_out = cotangent[0].astype(jnp.float32)
    grad_ffn = grad_out.astype(jnp.bfloat16)
    grad_ffn_rows = lax.all_gather(grad_ffn, "seq", axis=0, tiled=True)
    down_term = jnp.einsum("tf,td->fd", mixed, grad_ffn_rows, preferred_element_type=jnp.float32)
    grad_mixed = jnp.einsum(
        "td,fd->tf", grad_ffn_rows, down_weight, preferred_element_type=jnp.float32
    )
    grad_gate = (grad_mixed * upward * sigmoid_gate * (1.0 + gate * (1.0 - sigmoid_gate))).astype(
        jnp.bfloat16
    )
    grad_upward = (grad_mixed * activated).astype(jnp.bfloat16)
    gate_term = jnp.einsum(
        "td,tf->df", normed_two_rows, grad_gate, preferred_element_type=jnp.float32
    )
    up_term = jnp.einsum(
        "td,tf->df", normed_two_rows, grad_upward, preferred_element_type=jnp.float32
    )
    grad_normed_two = lax.psum_scatter(
        jnp.einsum("tf,df->td", grad_gate, gate_weight, preferred_element_type=jnp.float32)
        + jnp.einsum("tf,df->td", grad_upward, up_weight, preferred_element_type=jnp.float32),
        "seq",
        scatter_dimension=0,
        tiled=True,
    )
    feed_gain_term, grad_hidden_norm = norm_backward(
        hidden, scale_two, feedforward_gain, grad_normed_two
    )
    grad_hidden = grad_out + grad_hidden_norm
    grad_branch = grad_hidden.astype(jnp.bfloat16)
    grad_branch_rows = lax.all_gather(grad_branch, "seq", axis=0, tiled=True)
    out_term = jnp.einsum(
        "te,td->ed", attended, grad_branch_rows, preferred_element_type=jnp.float32
    )
    grad_attended = jnp.einsum(
        "td,ed->te", grad_branch_rows, out_weight, preferred_element_type=jnp.float32
    ).astype(jnp.bfloat16)
    grad_heads = grad_attended.reshape(group_rows, kv_local, head_share, HD)
    grad_keys = jnp.zeros((group_rows, kv_local, HD), jnp.float32)
    grad_values = jnp.zeros((group_rows, kv_local, HD), jnp.float32)
    grad_query_blocks = []
    for block_index in range(group_rows // block_rows):
        row_first = block_index * block_rows
        row_last = row_first + block_rows
        query_block = query_heads[row_first:row_last]
        query_starts = starts[row_first:row_last]
        grad_block = grad_heads[row_first:row_last]
        lse_block = lse_blocks[block_index]
        grad_query, grad_key, grad_value = block_backward(
            query_block, key_heads, value_heads, grad_block, lse_block, query_starts, row_first, 0
        )
        grad_query_blocks.append(grad_query)
        grad_keys = grad_keys + grad_key
        grad_values = grad_values + grad_value
    grad_query_rot = (
        jnp.concatenate(grad_query_blocks, axis=0)
        .astype(jnp.bfloat16)
        .astype(jnp.float32)
        .reshape(group_rows, heads_local, HD)
    )
    grad_key_rot = grad_keys.astype(jnp.bfloat16).astype(jnp.float32)
    grad_value_act = grad_values.astype(jnp.bfloat16).reshape(group_rows, kv_local * HD)
    grad_query_pre = (
        rotate_back(grad_query_rot, cosine_table, sine_table)
        .reshape(group_rows, heads_local * HD)
        .astype(jnp.bfloat16)
    )
    grad_key_pre = (
        rotate_back(grad_key_rot, cosine_table, sine_table)
        .reshape(group_rows, kv_local * HD)
        .astype(jnp.bfloat16)
    )
    query_term = jnp.einsum(
        "td,te->de", normed_rows, grad_query_pre, preferred_element_type=jnp.float32
    )
    key_term = jnp.einsum(
        "td,te->de", normed_rows, grad_key_pre, preferred_element_type=jnp.float32
    )
    value_term = jnp.einsum(
        "td,te->de", normed_rows, grad_value_act, preferred_element_type=jnp.float32
    )
    total = jnp.einsum(
        "te,de->td", grad_query_pre, query_weight, preferred_element_type=jnp.float32
    )
    total = total + jnp.einsum(
        "te,de->td", grad_key_pre, key_weight, preferred_element_type=jnp.float32
    )
    grad_normed_one = lax.psum_scatter(
        total
        + jnp.einsum("te,de->td", grad_value_act, value_weight, preferred_element_type=jnp.float32),
        "seq",
        scatter_dimension=0,
        tiled=True,
    )
    attention_gain_term, grad_inputs_norm = norm_backward(
        inputs, scale_one, attention_gain, grad_normed_one
    )
    input_grad = grad_hidden + grad_inputs_norm
    gain_sums = (
        lax.psum_scatter(attention_gain_term, ("seq", "batch"), scatter_dimension=0, tiled=True),
        lax.psum_scatter(feed_gain_term, ("seq", "batch"), scatter_dimension=0, tiled=True),
    )
    every_sum = (
        lax.psum_scatter(
            query_term.astype(jnp.bfloat16), "batch", scatter_dimension=0, tiled=True
        ).astype(jnp.float32),
        lax.psum_scatter(
            key_term.astype(jnp.bfloat16), "batch", scatter_dimension=0, tiled=True
        ).astype(jnp.float32),
        lax.psum_scatter(
            value_term.astype(jnp.bfloat16), "batch", scatter_dimension=0, tiled=True
        ).astype(jnp.float32),
        lax.psum_scatter(
            out_term.astype(jnp.bfloat16), "batch", scatter_dimension=0, tiled=True
        ).astype(jnp.float32),
        lax.psum_scatter(
            gate_term.astype(jnp.bfloat16), "batch", scatter_dimension=0, tiled=True
        ).astype(jnp.float32),
        lax.psum_scatter(
            up_term.astype(jnp.bfloat16), "batch", scatter_dimension=0, tiled=True
        ).astype(jnp.float32),
        lax.psum_scatter(
            down_term.astype(jnp.bfloat16), "batch", scatter_dimension=0, tiled=True
        ).astype(jnp.float32),
    )
    attention_sums = every_sum[:4]
    feed_sums = every_sum[4:]
    return (
        layer_out.reshape(1, local_rows, model_width),
        input_grad.reshape(1, local_rows, model_width),
        attention_sums[0],
        attention_sums[1],
        attention_sums[2],
        attention_sums[3],
        feed_sums[0],
        feed_sums[1],
        feed_sums[2],
        gain_sums[0],
        gain_sums[1],
    )


def solution(mesh):
    return jax.shard_map(
        shards,
        mesh=mesh,
        in_specs=(
            P("batch", "seq", None),
            P("batch"),
            P(None, "seq"),
            P(None, "seq"),
            P(None, "seq"),
            P("seq", None),
            P(None, "seq"),
            P(None, "seq"),
            P("seq", None),
            P(),
            P(),
            P("batch", "seq", None),
        ),
        out_specs=(
            P("batch", "seq", None),
            P("batch", "seq", None),
            P("batch", "seq"),
            P("batch", "seq"),
            P("batch", "seq"),
            P(("seq", "batch"), None),
            P("batch", "seq"),
            P("batch", "seq"),
            P(("seq", "batch"), None),
            P(("seq", "batch")),
            P(("seq", "batch")),
        ),
        check_vma=False,
    )
```

profile of v0, /device:TPU:0, one launch (start us, length us, event | category | flops | bytes accessed | tf_op | source)
XLA Modules:
  0.0 1025.1 jit_solution(4431347114280792653)
XLA Ops:
  10.1 2.5 fusion.30
  14.9 53.2 %all-gather.6.cloned.1.call-done = bf16[1024,2048]{1,0:T(8,128)(2,1)} async-done(((bf16[256,2048]{1,0:T(8,128)(2,1)}), bf16[1024,2048]{1,0:T(8,128)(2,1)}) %all-gather.6.cloned.1.call-update) | async-done | bytes 4194320 | tf_op jit(solution)/shard_map/all_gather | solution.py:157
  68.1 3.7 convolution_bitcast_fusion.1
  72.4 4.1 fusion.117
  83.4 7.5 fusion.115
  90.9 8.0 fusion.3
  98.9 7.4 fusion.44
  107.1 5.6 fusion.73
  112.8 86.4 %reduce-scatter.12.cloned.1.call-done = f32[256,2048]{1,0:T(8,128)} async-done(((f32[1024,2048]{1,0:T(8,128)}), f32[256,2048]{1,0:T(8,128)}) %reduce-scatter.12.cloned.1.call-update) | async-done | bytes 2097168 | tf_op jit(solution)/shard_map/reduce_scatter | solution.py:190
  204.4 52.1 %all-gather.8.cloned.1.call-done = bf16[1024,2048]{1,0:T(8,128)(2,1)} async-done(((bf16[256,2048]{1,0:T(8,128)(2,1)}), bf16[1024,2048]{1,0:T(8,128)(2,1)}) %all-gather.8.cloned.1.call-update) | async-done | bytes 4194320 | tf_op jit(solution)/shard_map/all_gather | solution.py:199
  256.5 12.1 %fusion.119 = f32[1024,1408]{1,0:T(8,128)} fusion(bf16[1024,2048]{1,0:T(8,128)(2,1)} %all-gather.8.cloned.1.call-done, bf16[2048,1408]{1,0:T(8,128)(2,1)} %param.19), kind=kOutput, calls=%fused_computation.180 | convolution fusion | flops 5905580032 | bytes 15728640 | tf_op jit(solution)/shard_map/dot_general | solution.py:201
  268.6 10.3 %fusion.118 = f32[1024,1408]{1,0:T(8,128)} fusion(bf16[1024,2048]{1,0:T(8,128)(2,1)S(1)} %copy-done.44, bf16[2048,1408]{1,0:T(8,128)(2,1)} %param.18), kind=kOutput, calls=%fused_computation.179 | convolution fusion | flops 5905580032 | bytes 15728640 | tf_op jit(solution)/shard_map/dot_general | solution.py:200
  278.9 31.9 %all-gather.12.cloned.1.call-done = bf16[1,1024,2048]{2,1,0:T(8,128)(2,1)} async-done(((bf16[1,256,2048]{2,1,0:T(8,128)(2,1)}), bf16[1,1024,2048]{2,1,0:T(8,128)(2,1)}) %all-gather.12.cloned.1.call-update) | async-done | bytes 4194320 | tf_op jit(solution)/shard_map/all_gather | solution.py:214
  310.8 15.6 %multiply_convert_fusion = (bf16[1024,1408]{1,0:T(8,128)(2,1)S(1)}, bf16[1024,1408]{1,0:T(8,128)(2,1)S(1)}, bf16[1024,1408]{1,0:T(8,128)(2,1)}) fusion(f32[1024,1408]{1,0:T(8,128)} %fusion.118, f32[1024,1408]{1,0:T(8,128)} %fusion.119, bf16[1408,2048]{1,0:T(8,128)(2,1)} %param.20, bf16[1,1024,2048]{2,1,0:T(8,128)(2,1)} %all-gather.12.cloned.1.call-done), kind=kOutput, calls=%fused_computation.32 | convolution fusion | flops 5927206912 | bytes 30146560 | tf_op jit(solution)/shard_map/td,fd->tf/dot_general | solution.py:216
  326.4 10.8 %fusion.120 = f32[1024,2048]{1,0:T(8,128)S(1)} fusion(bf16[1024,1408]{1,0:T(8,128)(2,1)S(1)} %get-tuple-element.22, bf16[2048,1408]{1,0:T(8,128)(2,1)} %param.18), kind=kOutput, calls=%fused_computation.181 | convolution fusion | flops 5905580032 | bytes 17039360 | tf_op jit(solution)/shard_map/tf,df->td/dot_general | solution.py:230
  337.2 11.1 %convolution_add_fusion = f32[1024,2048]{1,0:T(8,128)} fusion(f32[1024,2048]{1,0:T(8,128)S(1)} %fusion.120, bf16[1024,1408]{1,0:T(8,128)(2,1)S(1)} %get-tuple-element.21, bf16[2048,1408]{1,0:T(8,128)(2,1)} %param.19), kind=kOutput, calls=%fused_computation.52 | convolution fusion | flops 5907677184 | bytes 25427968 | tf_op jit(solution)/shard_map/tf,df->td/dot_general | solution.py:231
  348.4 10.9 %convolution_convert_fusion.3 = bf16[1024,2048]{1,0:T(8,128)(2,1)} fusion(bf16[1024,1408]{1,0:T(8,128)(2,1)} %get-tuple-element.23, bf16[1408,2048]{1,0:T(8,128)(2,1)} %param.20), kind=kOutput, calls=%fused_computation.53 | convolution fusion | flops 5907677184 | bytes 12845056 | tf_op jit(solution)/shard_map/dot_general | solution.py:206
  359.5 75.4 %reduce-scatter.16.cloned.1.call-done = f32[256,2048]{1,0:T(8,128)} async-done(((f32[1024,2048]{1,0:T(8,128)}), f32[256,2048]{1,0:T(8,128)}) %reduce-scatter.16.cloned.1.call-update) | async-done | bytes 2097168 | tf_op jit(solution)/shard_map/reduce_scatter | solution.py:229
  434.9 3.4 multiply_reduce_fusion
  438.2 52.1 %reduce-scatter.14.cloned.1.call-done = bf16[256,2048]{1,0:T(8,128)(2,1)} async-done(((bf16[1024,2048]{1,0:T(8,128)(2,1)}), bf16[256,2048]{1,0:T(8,128)(2,1)}) %reduce-scatter.14.cloned.1.call-update) | async-done | bytes 1048592 | tf_op jit(solution)/shard_map/reduce_scatter | solution.py:205
  490.3 5.3 fusion.112
  495.7 10.6 %convolution_convert_fusion = bf16[1408,2048]{1,0:T(8,128)(2,1)} fusion(bf16[1024,1408]{1,0:T(8,128)(2,1)} %get-tuple-element.23, bf16[1,1024,2048]{2,1,0:T(8,128)(2,1)} %all-gather.12.cloned.1.call-done), kind=kOutput, calls=%fused_computation.27 | convolution fusion | flops 5908463616 | bytes 12845056 | tf_op jit(solution)/shard_map/tf,td->fd/dot_general | solution.py:215
  506.3 11.0 %convolution_convert_fusion.1 = bf16[2048,1408]{1,0:T(8,128)(2,1)} fusion(bf16[1024,2048]{1,0:T(8,128)(2,1)} %all-gather.8.cloned.1.call-done, bf16[1024,1408]{1,0:T(8,128)(2,1)} %copy-done.49), kind=kOutput, calls=%fused_computation.28 | convolution fusion | flops 5908463616 | bytes 12845056 | tf_op jit(solution)/shard_map/td,tf->df/dot_general | solution.py:226
  517.3 11.1 %convolution_convert_fusion.2 = bf16[2048,1408]{1,0:T(8,128)(2,1)} fusion(bf16[1024,2048]{1,0:T(8,128)(2,1)} %all-gather.8.cloned.1.call-done, bf16[1024,1408]{1,0:T(8,128)(2,1)} %copy-done.50), kind=kOutput, calls=%fused_computation.29 | convolution fusion | flops 5908463616 | bytes 12845056 | tf_op jit(solution)/shard_map/td,tf->df/dot_general | solution.py:223
  529.3 19.1 %all-gather.10.cloned.1.call-done = bf16[1024,2048]{1,0:T(8,128)(2,1)} async-done(((bf16[256,2048]{1,0:T(8,128)(2,1)}), bf16[1024,2048]{1,0:T(8,128)(2,1)}) %all-gather.10.cloned.1.call-update) | async-done | bytes 4194320 | tf_op jit(solution)/shard_map/all_gather | solution.py:241
  548.4 4.5 convolution_convert_fusion.8
  553.0 8.4 fusion.9
  561.4 7.2 fusion.21
  570.1 6.3 fusion.63
  576.9 2.9 fusion.68
  579.7 3.8 convolution_convert_fusion.6
  583.5 11.7 %fusion = (f32[8,512]{1,0:T(8,128)}, f32[1024,512,8]{1,0,2:T(8,128)}) fusion(f32[1,8,512,1024]{2,3,1,0:T(8,128)} %get-tuple-element.44, f32[8,512]{1,0:T(8,128)S(1)} %log_add_fusion, bf16[512,8,64]{0,2,1:T(8,128)(2,1)} %bitcast.247, bf16[1024,64]{0,1:T(8,128)(2,1)S(1)} %convolution_convert_fusion.9), kind=kOutput, calls=%fused_computation.3 | convolution fusion | flops 549449728 | bytes 34242560 | tf_op jit(solution)/shard_map/qngd,knd->ngqk/dot_general | solution.py:104
  595.4 12.3 %fusion.8 = bf16[8,512,1024]{1,2,0:T(8,128)(2,1)S(1)} fusion(f32[1024,512,8]{1,0,2:T(8,128)} %get-tuple-element.48, f32[1,8,512,1024]{2,3,1,0:T(8,128)} %get-tuple-element.44, f32[8,512]{1,0:T(8,128)} %get-tuple-element.47, f32[8,512]{1,0:T(8,128)S(1)} %log_add_fusion), kind=kLoop, calls=%fused_computation.13 | loop fusion | flops 16777216 | bytes 41975808 | tf_op jit(solution)/shard_map/reshape.58
  607.7 2.6 fusion.62
  614.6 6.1 convolution_convert_fusion.4
  621.0 3.6 fusion.48
  624.6 5.0 fusion.47
  632.2 3.8 convolution_convert_fusion.5
  640.4 4.6 add_add_fusion
  647.6 33.5 %reduce-scatter.30.cloned.1.call-done = bf16[256,1408]{1,0:T(8,128)(2,1)} async-done(((bf16[2048,1408]{1,0:T(8,128)(2,1)}), bf16[256,1408]{1,0:T(8,128)(2,1)}) %reduce-scatter.30.cloned.1.call-update) | async-done | bytes 720912 | tf_op jit(solution)/shard_map/reduce_scatter | solution.py:329
  683.4 63.1 %reduce-scatter.28.cloned.1.call-done = bf16[256,1408]{1,0:T(8,128)(2,1)} async-done(((bf16[2048,1408]{1,0:T(8,128)(2,1)}), bf16[256,1408]{1,0:T(8,128)(2,1)}) %reduce-scatter.28.cloned.1.call-update) | async-done | bytes 720912 | tf_op jit(solution)/shard_map/reduce_scatter | solution.py:326
  748.8 29.8 %reduce-scatter.24.cloned.1.call-done = bf16[256,64]{0,1:T(8,128)(2,1)} async-done(((bf16[2048,64]{0,1:T(8,128)(2,1)}), bf16[256,64]{0,1:T(8,128)(2,1)}) %reduce-scatter.24.cloned.1.call-update) | async-done | bytes 32784 | tf_op jit(solution)/shard_map/reduce_scatter | solution.py:320
  779.9 30.2 %reduce-scatter.22.cloned.1.call-done = bf16[256,64]{0,1:T(8,128)(2,1)} async-done(((bf16[2048,64]{0,1:T(8,128)(2,1)}), bf16[256,64]{0,1:T(8,128)(2,1)}) %reduce-scatter.22.cloned.1.call-update) | async-done | bytes 32784 | tf_op jit(solution)/shard_map/reduce_scatter | solution.py:317
  811.6 34.9 %reduce-scatter.26.cloned.1.call-done = bf16[64,2048]{1,0:T(8,128)(2,1)} async-done(((bf16[512,2048]{1,0:T(8,128)(2,1)}), bf16[64,2048]{1,0:T(8,128)(2,1)}) %reduce-scatter.26.cloned.1.call-update) | async-done | bytes 262160 | tf_op jit(solution)/shard_map/reduce_scatter | solution.py:323
  848.3 35.0 %reduce-scatter.20.cloned.1.call-done = bf16[256,512]{1,0:T(8,128)(2,1)} async-done(((bf16[2048,512]{1,0:T(8,128)(2,1)}), bf16[256,512]{1,0:T(8,128)(2,1)}) %reduce-scatter.20.cloned.1.call-update) | async-done | bytes 262160 | tf_op jit(solution)/shard_map/reduce_scatter | solution.py:314
  885.1 86.1 %reduce-scatter.18.cloned.1.call-done = f32[256,2048]{1,0:T(8,128)} async-done(((f32[1024,2048]{1,0:T(8,128)}), f32[256,2048]{1,0:T(8,128)}) %reduce-scatter.18.cloned.1.call-update) | async-done | bytes 2097168 | tf_op jit(solution)/shard_map/reduce_scatter | solution.py:298
  973.4 39.5 %all-reduce.4 = (f32[2048]{0:T(1024)S(1)}, f32[2048]{0:T(1024)S(1)}) all-reduce(f32[2048]{0:T(1024)S(1)} %get-tuple-element.13, f32[2048]{0:T(1024)S(1)} %copy-done.38), channel_id=14, replica_groups=mesh['seq'=4,'batch'=8] {'seq','batch'}, use_global_device_ids=true, to_apply=%region_22.23.clone | all-reduce | flops 4096 | bytes 32768
  1014.0 4.1 fusion.34
  (183 shorter events, 48.9 us)
Async XLA Ops:
  7.2 99.9 %copy-start = (bf16[512,2048]{1,0:T(8,128)(2,1)S(1)}, bf16[512,2048]{1,0:T(8,128)(2,1)}, u32[]{:S(2)}) copy-start(bf16[512,2048]{1,0:T(8,128)(2,1)} %param.17) | copy-start | bytes 6291460
  7.2 60.9 %copy-start.26 = (bf16[2048,64]{0,1:T(8,128)(2,1)S(1)}, bf16[2048,64]{0,1:T(8,128)(2,1)}, u32[]{:S(2)}) copy-start(bf16[2048,64]{0,1:T(8,128)(2,1)} %param.15) | copy-start | bytes 786436
  7.2 60.9 %all-gather.6.cloned.1.call-start = ((), (), s32[]{:S(2)}) async-start(), calls=%async_computation.11 | async-start | bytes 5242880 | tf_op jit(solution)/shard_map/all_gather | solution.py:157
  12.7 186.6 %reduce-scatter.12.cloned.1.call-start = ((), (), s32[]{:S(2)}) async-start(), calls=%async_computation.12 | async-start | bytes 10485760 | tf_op jit(solution)/shard_map/reduce_scatter | solution.py:190
  13.4 63.1 %copy-start.41 = (f32[32]{0:T(128)}, f32[32]{0:T(128)S(1)}, u32[]{:S(2)}) copy-start(f32[32]{0:T(128)S(1)} %multiply_exponential_fusion) | copy-start | bytes 388
  13.5 63.0 %copy-start.32 = (f32[1024]{0:T(1024)}, f32[1024]{0:T(1024)S(1)}, u32[]{:S(2)}) copy-start(f32[1024]{0:T(1024)S(1)} %subtract_convert_fusion.2) | copy-start | bytes 12292
  14.4 62.2 %copy-start.16 = (f32[1024,32]{0,1:T(8,128)}, f32[1024,32]{0,1:T(8,128)S(1)}, u32[]{:S(2)}) copy-start(f32[1024,32]{0,1:T(8,128)S(1)} %get-tuple-element.35) | copy-start | bytes 393220
  14.4 62.2 %copy-start.18 = (f32[1024,32]{0,1:T(8,128)}, f32[1024,32]{0,1:T(8,128)S(1)}, u32[]{:S(2)}) copy-start(f32[1024,32]{0,1:T(8,128)S(1)} %get-tuple-element.36) | copy-start | bytes 393220
  72.4 10.9 %copy-start.20 = (bf16[1024,1,32]{0,2,1:T(8,128)(2,1)}, bf16[1024,1,32]{0,2,1:T(8,128)(2,1)S(1)}, u32[]{:S(2)}) copy-start(bf16[1024,1,32]{0,2,1:T(8,128)(2,1)S(1)} %get-tuple-element.33) | copy-start | bytes 196612
  72.4 10.9 %copy-start.22 = (bf16[1024,1,32]{0,2,1:T(8,128)(2,1)}, bf16[1024,1,32]{0,2,1:T(8,128)(2,1)S(1)}, u32[]{:S(2)}) copy-start(bf16[1024,1,32]{0,2,1:T(8,128)(2,1)S(1)} %get-tuple-element.34) | copy-start | bytes 196612
  76.9 6.4 copy-start.10
  76.9 6.4 copy-start.12
  83.3 23.0 %copy-start.46 = (bf16[64,8,512]{2,0,1:T(8,128)(2,1)}, bf16[64,8,512]{2,0,1:T(8,128)(2,1)S(1)}, u32[]{:S(2)}) copy-start(bf16[64,8,512]{2,0,1:T(8,128)(2,1)S(1)} %fusion.41) | copy-start | bytes 1572868
  112.8 86.5 %copy-start.8 = (bf16[1,256,2048]{2,1,0:T(8,128)(2,1)S(1)}, bf16[1,256,2048]{2,1,0:T(8,128)(2,1)}, u32[]{:S(2)}) copy-start(bf16[1,256,2048]{2,1,0:T(8,128)(2,1)} %param.12) | copy-start | bytes 3145732
  112.8 89.7 %copy-start.31 = (f32[2048]{0:T(1024)S(1)}, f32[2048]{0:T(1024)}, u32[]{:S(2)}) copy-start(f32[2048]{0:T(1024)} %param.22) | copy-start | bytes 24580
  112.8 143.7 %all-gather.8.cloned.1.call-start = ((), (), s32[]{:S(2)}) async-start(), calls=%async_computation.13 | async-start | bytes 5242880 | tf_op jit(solution)/shard_map/all_gather | solution.py:199
  203.8 107.0 %all-gather.12.cloned.1.call-start = ((), (), s32[]{:S(2)}) async-start(), calls=%async_computation.25 | async-start | bytes 5242880 | tf_op jit(solution)/shard_map/all_gather | solution.py:214
  204.3 230.5 %reduce-scatter.16.cloned.1.call-start = ((), (), s32[]{:S(2)}) async-start(), calls=%async_computation.15 | async-start | bytes 10485760 | tf_op jit(solution)/shard_map/reduce_scatter | solution.py:229
  256.5 12.1 %copy-start.44 = (bf16[1024,2048]{1,0:T(8,128)(2,1)S(1)}, bf16[1024,2048]{1,0:T(8,128)(2,1)}, u32[]{:S(2)}) copy-start(bf16[1024,2048]{1,0:T(8,128)(2,1)} %all-gather.8.cloned.1.call-done) | copy-start | bytes 12582916
  326.4 10.8 %copy-start.50 = (bf16[1024,1408]{1,0:T(8,128)(2,1)}, bf16[1024,1408]{1,0:T(8,128)(2,1)S(1)}, u32[]{:S(2)}) copy-start(bf16[1024,1408]{1,0:T(8,128)(2,1)S(1)} %get-tuple-element.22) | copy-start | bytes 8650756
  326.4 10.8 %copy-start.49 = (bf16[1024,1408]{1,0:T(8,128)(2,1)}, bf16[1024,1408]{1,0:T(8,128)(2,1)S(1)}, u32[]{:S(2)}) copy-start(bf16[1024,1408]{1,0:T(8,128)(2,1)S(1)} %get-tuple-element.21) | copy-start | bytes 8650756
  348.4 141.9 %reduce-scatter.14.cloned.1.call-start = ((), (), s32[]{:S(2)}) async-start(), calls=%async_computation.14 | async-start | bytes 5242880 | tf_op jit(solution)/shard_map/reduce_scatter | solution.py:205
  359.4 130.9 %copy-start.15 = (bf16[1,256,2048]{2,1,0:T(8,128)(2,1)S(1)}, bf16[1,256,2048]{2,1,0:T(8,128)(2,1)}, u32[]{:S(2)}) copy-start(bf16[1,256,2048]{2,1,0:T(8,128)(2,1)} %param.23) | copy-start | bytes 3145732
  359.4 188.9 %all-gather.10.cloned.1.call-start = ((), (), s32[]{:S(2)}) async-start(), calls=%async_computation.16 | async-start | bytes 5242880 | tf_op jit(solution)/shard_map/all_gather | solution.py:241
  495.6 149.5 %reduce-scatter.32.cloned.1.call-start = ((), (), s32[]{:S(2)}) async-start(), calls=%async_computation.24 | async-start | bytes 6488064 | tf_op jit(solution)/shard_map/reduce_scatter | solution.py:332
  506.3 174.8 %reduce-scatter.30.cloned.1.call-start = ((), (), s32[]{:S(2)}) async-start(), calls=%async_computation.23 | async-start | bytes 6488064 | tf_op jit(solution)/shard_map/reduce_scatter | solution.py:329
  517.3 229.2 %reduce-scatter.28.cloned.1.call-start = ((), (), s32[]{:S(2)}) async-start(), calls=%async_computation.22 | async-start | bytes 6488064 | tf_op jit(solution)/shard_map/reduce_scatter | solution.py:326
  528.5 250.0 %reduce-scatter.24.cloned.1.call-start = ((), (), s32[]{:S(2)}) async-start(), calls=%async_computation.20 | async-start | bytes 294912 | tf_op jit(solution)/shard_map/reduce_scatter | solution.py:320
  553.0 23.4 %copy-start.14 = (bf16[512,512]{0,1:T(8,128)(2,1)}, bf16[512,512]{0,1:T(8,128)(2,1)S(1)}, u32[]{:S(2)}) copy-start(bf16[512,512]{0,1:T(8,128)(2,1)S(1)} %get-tuple-element.30) | copy-start | bytes 1572868
  561.4 7.3 copy-start.11
  561.4 7.3 copy-start.13
  561.4 15.0 %slice-start = ((s8[16777216]{0:T(1024)(128)(4,1)}), s8[4194304]{0:T(1024)(128)(4,1)S(1)}, s32[]{:S(2)}) async-start(s8[16777216]{0:T(1024)(128)(4,1)} %bitcast.244), calls=%async_computation.26 | async-start | bytes 8388608
  561.4 15.0 %slice-start.1 = ((s8[16777216]{0:T(1024)(128)(4,1)}), s8[4194304]{0:T(1024)(128)(4,1)S(1)}, s32[]{:S(2)}) async-start(s8[16777216]{0:T(1024)(128)(4,1)} %bitcast.244), calls=%async_computation.27 | async-start | bytes 8388608
  561.4 15.0 %slice-start.2 = ((s8[16777216]{0:T(1024)(128)(4,1)}), s8[4194304]{0:T(1024)(128)(4,1)S(1)}, s32[]{:S(2)}) async-start(s8[16777216]{0:T(1024)(128)(4,1)} %bitcast.244), calls=%async_computation.28 | async-start | bytes 8388608
  568.7 7.7 copy-start.6
  570.1 6.8 slice-start.3
  595.3 214.9 %reduce-scatter.22.cloned.1.call-start = ((), (), s32[]{:S(2)}) async-start(), calls=%async_computation.19 | async-start | bytes 294912 | tf_op jit(solution)/shard_map/reduce_scatter | solution.py:317
  614.5 6.5 copy-start.21
  614.5 6.5 copy-start.23
  614.5 232.0 %reduce-scatter.26.cloned.1.call-start = ((), (), s32[]{:S(2)}) async-start(), calls=%async_computation.21 | async-start | bytes 2359296 | tf_op jit(solution)/shard_map/reduce_scatter | solution.py:323
  620.7 262.6 %reduce-scatter.20.cloned.1.call-start = ((), (), s32[]{:S(2)}) async-start(), calls=%async_computation.18 | async-start | bytes 2359296 | tf_op jit(solution)/shard_map/reduce_scatter | solution.py:314
  624.6 5.3 copy-start.17
  636.0 335.2 %reduce-scatter.18.cloned.1.call-start = ((), (), s32[]{:S(2)}) async-start(), calls=%async_computation.17 | async-start | bytes 10485760 | tf_op jit(solution)/shard_map/reduce_scatter | solution.py:298
  645.1 326.2 %copy-start.9 = (bf16[1,256,2048]{2,1,0:T(8,128)(2,1)S(1)}, bf16[1,256,2048]{2,1,0:T(8,128)(2,1)}, u32[]{:S(2)}) copy-start(bf16[1,256,2048]{2,1,0:T(8,128)(2,1)} %param.12) | copy-start | bytes 3145732
  645.1 326.1 %copy-start.30 = (f32[2048]{0:T(1024)S(1)}, f32[2048]{0:T(1024)}, u32[]{:S(2)}) copy-start(f32[2048]{0:T(1024)} %param.21) | copy-start | bytes 24580
  645.1 326.1 %copy-start.40 = (f32[256]{0:T(256)S(1)}, f32[256]{0:T(256)}, u32[]{:S(2)}) copy-start(f32[256]{0:T(256)} %copy-done.39) | copy-start | bytes 3076
  647.6 325.8 %copy-start.38 = (f32[2048]{0:T(1024)S(1)}, f32[2048]{0:T(1024)}, u32[]{:S(2)}) copy-start(f32[2048]{0:T(1024)} %get-tuple-element.11) | copy-start | bytes 24580
  647.6 366.4 %copy-start.43 = (f32[256]{0:T(256)S(1)}, f32[256]{0:T(256)}, u32[]{:S(2)}) copy-start(f32[256]{0:T(256)} %get-tuple-element.39) | copy-start | bytes 3076
  (22 other events, 59.1 us)
Sparse Core Ops, SparseCore 0:
  12.8 55.2 all-gather.5
  112.9 86.3 reduce-scatter.11
  203.9 52.5 all-gather.7
  258.2 52.5 all-gather.11
  348.5 86.3 reduce-scatter.15
  437.7 52.5 reduce-scatter.13
  495.8 52.5 all-gather.9
  550.7 64.7 reduce-scatter.31
  617.8 63.2 reduce-scatter.29
  683.2 63.2 reduce-scatter.27
  749.3 29.1 reduce-scatter.23
  781.2 28.9 reduce-scatter.21
  812.5 34.0 reduce-scatter.25
  848.7 34.5 reduce-scatter.19
  886.2 84.9 reduce-scatter.17
where the time goes:
time: 1030 us
  waiting for transfers between devices  684 us (66%)
  matrix products  206 us (20%)
  other arithmetic  68.6 us (7%)
  blocking collectives  39.5 us (4%)
  between operations  15.8 us (2%)
  local copies, waits for them, and re-layouts  10.5 us (1%)
    reduce_scatter x1, waiting for transfers between devices, shards(): lax.psum_scatter(jnp.dot(attended, out_weight, preferred_element_type=jnp...  86.4 us
    reduce_scatter x1, waiting for transfers between devices, shards(): lax.psum_scatter(total + jnp.einsum('te,de->td', grad_value_act, value_we...  86.1 us
    reduce_scatter x1, waiting for transfers between devices, shards(): lax.psum_scatter(jnp.einsum('tf,df->td', grad_gate, gate_weight, preferre...  75.4 us
    reduce_scatter x1, waiting for transfers between devices, shards(): lax.psum_scatter(gate_term.astype(jnp.bfloat16), 'batch', scatter_dimensi...  63.1 us
    all_gather x1, waiting for transfers between devices, shards(): normed_rows = lax.all_gather(normed_one, 'seq', axis=0, tiled=True)  53.2 us
    all_gather x1, waiting for transfers between devices, shards(): normed_two_rows = lax.all_gather(normed_two, 'seq', axis=0, tiled=True)  52.1 us
    reduce_scatter x1, waiting for transfers between devices, shards(): lax.psum_scatter(jnp.dot(mixed, down_weight, preferred_element_type=jnp.f...  52.1 us
    unnamed x1, blocking collectives  39.5 us
  transfers between devices with their start and end apart: 15, of which 14 were waited for; matrix products, arithmetic and copies ran while one was open for 17% of the time, Pallas kernels for 0%

commit v1 on v0

v1 whole, which is shorter than its diff:
```python
import math

import jax
import jax.numpy as jnp
from jax import lax
from jax.experimental import pallas as pl
from jax.experimental.pallas import tpu as pltpu
from jax.sharding import PartitionSpec as P

HD = 64
EPS = 1e-05
NEG = -1e30
F32 = jnp.float32
BF16 = jnp.bfloat16


def mm(a, b):
    return lax.dot_general(a, b, (((1,), (0,)), ((), ())), preferred_element_type=F32)


def mm_nt(a, b):
    return lax.dot_general(a, b, (((1,), (1,)), ((), ())), preferred_element_type=F32)


def mm_tn(a, b):
    return lax.dot_general(a, b, (((0,), (0,)), ((), ())), preferred_element_type=F32)


def exchange(values, even_mask, odd_mask):
    seq_parts = lax.axis_size("seq")
    batch_parts = lax.axis_size("batch")
    pairs = []
    for part in range(seq_parts):
        for group in range(batch_parts):
            mask = even_mask if group % 2 == 0 else odd_mask
            pairs.append((part * batch_parts + group, (part ^ mask) * batch_parts + group))
    return lax.ppermute(values, ("seq", "batch"), pairs)


def first_swap(values):
    return exchange(values, 1, 2)


def second_swap(values):
    return exchange(values, 2, 1)


def gather_blocks(block):
    near = first_swap(block)
    side = second_swap(block)
    far = second_swap(near)
    return [block, near, side, far]


def scatter_sum(upper, lower):
    rows = lower.shape[0] // 2
    arrived = second_swap(upper)
    passed = (lower[rows:].astype(F32) + arrived[rows:].astype(F32)).astype(BF16)
    last = first_swap(passed)
    return lower[:rows].astype(F32) + arrived[:rows].astype(F32) + last.astype(F32)


def swap_halves(values):
    lane = lax.broadcasted_iota(jnp.int32, values.shape, 1)
    ahead = pltpu.roll(values, values.shape[1] - HD // 2, 1)
    behind = pltpu.roll(values, HD // 2, 1)
    return jnp.where(lane % HD < HD // 2, ahead, behind)


def padded_keys(keys_values):
    lane = lax.broadcasted_iota(jnp.int32, keys_values.shape, 1)
    zero = jnp.zeros_like(keys_values)
    left = jnp.where(lane < HD, keys_values, zero)
    right = pltpu.roll(left, HD, 1)
    return jnp.concatenate([left, right], axis=0)


def padded_values(keys_values):
    lane = lax.broadcasted_iota(jnp.int32, keys_values.shape, 1)
    zero = jnp.zeros_like(keys_values)
    right = jnp.where(lane >= HD, keys_values, zero)
    left = pltpu.roll(right, HD, 1)
    return jnp.concatenate([left, right], axis=0)


def attention_forward_kernel(
    info, query_ref, kv_ref, cos_ref, sin_ref, cos_all, sin_all,
    attended_ref, rotated_ref, kv_out, lse_ref, keys_s, values_s, acc_s, max_s,
):
    step = pl.program_id(0)
    rows = query_ref.shape[0]
    pairs = query_ref.shape[1] // 128
    blocks = kv_ref.shape[0] // rows

    @pl.when(step == 0)
    def _():
        for part in range(blocks):
            here = pl.ds(part * rows, rows)
            kv = kv_ref[here, :]
            lane = lax.broadcasted_iota(jnp.int32, kv.shape, 1)
            turned = kv * cos_all[here, :] + swap_halves(kv) * sin_all[here, :]
            kv = jnp.where(lane < HD, turned, kv).astype(BF16).astype(F32)
            kv_out[here, :] = kv.astype(BF16)
            keys_s[part] = (padded_keys(kv) * (1.0 / math.sqrt(HD))).astype(BF16)
            both = padded_values(kv)
            lane2 = lax.broadcasted_iota(jnp.int32, both.shape, 1)
            row2 = lax.broadcasted_iota(jnp.int32, both.shape, 0)
            ones = jnp.where((lane2 < HD) == (row2 < rows), 1.0, 0.0)
            values_s[part] = jnp.concatenate([both, ones], axis=1).astype(BF16)

    own = info[step]
    low = info[2 * blocks + step]
    row = lax.broadcasted_iota(jnp.int32, (rows, rows), 0)
    column = lax.broadcasted_iota(jnp.int32, (rows, rows), 1)
    allowed = column <= row
    left_half = lax.broadcasted_iota(jnp.int32, (rows, 2 * 128), 1) % 128 < HD
    at = info[blocks + own]
    for pair in range(pairs):
        cols = pl.ds(pair * 128, 128)
        query = query_ref[:, cols]
        query = (query * cos_ref[...] + swap_halves(query) * sin_ref[...]).astype(BF16)
        rotated_ref[:, cols] = query
        scores = mm_nt(query, keys_s[at])
        probs = []
        for head in range(2):
            part = jnp.where(allowed, scores[:, head * rows : (head + 1) * rows], NEG)
            top = jnp.max(part, axis=1, keepdims=True)
            probs.append(jnp.exp(part - top))
            max_s[2 * pair + head] = jnp.broadcast_to(top, (rows, 128))
        acc_s[pair] = mm(jnp.concatenate(probs, axis=1).astype(BF16), values_s[at])

    for back in range(1, blocks):

        @pl.when(own - back >= low)
        def _():
            where_ = info[blocks + jnp.maximum(own - back, 0)]
            for pair in range(pairs):
                query = rotated_ref[:, pl.ds(pair * 128, 128)]
                scores = mm_nt(query, keys_s[where_])
                probs = []
                scale = []
                for head in range(2):
                    part = scores[:, head * rows : (head + 1) * rows]
                    before = max_s[2 * pair + head][:, :1]
                    top = jnp.maximum(before, jnp.max(part, axis=1, keepdims=True))
                    probs.append(jnp.exp(part - top))
                    scale.append(jnp.exp(before - top))
                    max_s[2 * pair + head] = jnp.broadcast_to(top, (rows, 128))
                factor = jnp.where(left_half, scale[0], scale[1])
                acc_s[pair] = acc_s[pair] * factor + mm(
                    jnp.concatenate(probs, axis=1).astype(BF16), values_s[where_]
                )

    lane = lax.broadcasted_iota(jnp.int32, (rows, 128), 1)
    logs = jnp.zeros((rows, 128), F32)
    for pair in range(pairs):
        total = acc_s[pair][:, 128:]
        attended_ref[:, pl.ds(pair * 128, 128)] = (acc_s[pair][:, :128] / total).astype(BF16)
        log_total = jnp.log(total)
        for head in range(2):
            value = max_s[2 * pair + head] + jnp.broadcast_to(
                log_total[:, head * HD : head * HD + 1], (rows, 128)
            )
            logs = jnp.where(lane == 2 * pair + head, value, logs)
    lse_ref[...] = jnp.transpose(logs)[: 2 * pairs, :]


def attention_forward(info, qkv, cosine, sine, rows):
    total, width = qkv.shape
    blocks = total // rows
    query_width = width - 2 * HD
    pairs = query_width // 128
    last = query_width // 128
    return pl.pallas_call(
        attention_forward_kernel,
        grid_spec=pltpu.PrefetchScalarGridSpec(
            num_scalar_prefetch=1,
            grid=(blocks,),
            in_specs=[
                pl.BlockSpec((rows, query_width), lambda j, info: (j, 0)),
                pl.BlockSpec((total, 128), lambda j, info: (0, last)),
                pl.BlockSpec((rows, 128), lambda j, info: (j, 0)),
                pl.BlockSpec((rows, 128), lambda j, info: (j, 0)),
                pl.BlockSpec((total, 128), lambda j, info: (0, 0)),
                pl.BlockSpec((total, 128), lambda j, info: (0, 0)),
            ],
            out_specs=[
                pl.BlockSpec((rows, query_width), lambda j, info: (j, 0)),
                pl.BlockSpec((rows, query_width), lambda j, info: (j, 0)),
                pl.BlockSpec((total, 128), lambda j, info: (0, 0)),
                pl.BlockSpec((2 * pairs, rows), lambda j, info: (0, j)),
            ],
            scratch_shapes=[
                pltpu.VMEM((blocks, 2 * rows, 128), BF16),
                pltpu.VMEM((blocks, 2 * rows, 256), BF16),
                pltpu.VMEM((pairs, rows, 256), F32),
                pltpu.VMEM((2 * pairs, rows, 128), F32),
            ],
        ),
        out_shape=[
            jax.ShapeDtypeStruct((total, query_width), BF16),
            jax.ShapeDtypeStruct((total, query_width), BF16),
            jax.ShapeDtypeStruct((total, 128), BF16),
            jax.ShapeDtypeStruct((2 * pairs, total), F32),
        ],
        name="attention_forward",
    )(info, qkv, qkv, cosine, sine, cosine, sine)


def attention_backward_kernel(
    info, query_ref, att_ref, grad_ref, lse_ref, kv_ref, cos_ref, sin_ref, cos_all, sin_all,
    out_ref, keys_s, values_s, key_acc, value_acc, query_acc, delta_s,
):
    step = pl.program_id(0)
    rows = query_ref.shape[0]
    query_width = query_ref.shape[1]
    pairs = query_width // 128
    blocks = kv_ref.shape[0] // rows

    @pl.when(step == 0)
    def _():
        for part in range(blocks):
            kv = kv_ref[pl.ds(part * rows, rows), :].astype(F32)
            keys_s[part] = (padded_keys(kv) * (1.0 / math.sqrt(HD))).astype(BF16)
            values_s[part] = padded_values(kv).astype(BF16)
        key_acc[...] = jnp.zeros_like(key_acc)
        value_acc[...] = jnp.zeros_like(value_acc)

    own = info[step]
    low = info[2 * blocks + step]
    at = info[blocks + own]
    key_index = lax.broadcasted_iota(jnp.int32, (2 * rows, rows), 0) % rows
    query_index = lax.broadcasted_iota(jnp.int32, (2 * rows, rows), 1)
    allowed = key_index <= query_index
    top_half = lax.broadcasted_iota(jnp.int32, (2 * rows, rows), 0) < rows

    products = att_ref[...].astype(F32) * grad_ref[...].astype(F32)
    head_row = lax.broadcasted_iota(jnp.int32, (2 * pairs, query_width), 0)
    head_col = lax.broadcasted_iota(jnp.int32, (2 * pairs, query_width), 1) // HD
    picker = jnp.where(head_row == head_col, 1.0, 0.0)
    delta_s[...] = lax.dot_general(
        picker, products, (((1,), (1,)), ((), ())),
        precision=lax.Precision.HIGHEST, preferred_element_type=F32,
    )

    def one_block(where_, masked):
        keys = keys_s[where_]
        values = values_s[where_]
        for pair in range(pairs):
            cols = pl.ds(pair * 128, 128)
            query = query_ref[:, cols]
            grad = grad_ref[:, cols]
            lse = jnp.where(
                top_half, lse_ref[2 * pair : 2 * pair + 1, :], lse_ref[2 * pair + 1 : 2 * pair + 2, :]
            )
            delta = jnp.where(
                top_half, delta_s[2 * pair : 2 * pair + 1, :], delta_s[2 * pair + 1 : 2 * pair + 2, :]
            )
            scores = mm_nt(keys, query) - lse
            if masked:
                scores = jnp.where(allowed, scores, NEG)
            probs = jnp.exp(scores)
            grad_probs = mm_nt(values, grad)
            grad_scores = (probs * (grad_probs - delta)).astype(BF16)
            value_acc[where_] += mm(probs.astype(BF16), grad)
            key_acc[where_] += mm(grad_scores, query)
            part = mm_tn(grad_scores, keys)
            if masked:
                query_acc[:, cols] = part
            else:
                query_acc[:, cols] += part

    one_block(at, True)
    for back in range(1, blocks):

        @pl.when(own - back >= low)
        def _():
            one_block(info[blocks + jnp.maximum(own - back, 0)], False)

    here = pl.ds(pl.multiple_of(step * rows, rows), rows)
    for pair in range(pairs):
        cols = pl.ds(pair * 128, 128)
        grad = query_acc[:, cols].astype(BF16).astype(F32)
        out_ref[here, cols] = (grad * cos_ref[...] - swap_halves(grad) * sin_ref[...]).astype(BF16)

    @pl.when(step == pl.num_programs(0) - 1)
    def _():
        lane = lax.broadcasted_iota(jnp.int32, (rows, 128), 1)
        for part in range(blocks):
            spot = pl.ds(part * rows, rows)
            key_grad = key_acc[part]
            key_grad = key_grad[:rows] + pltpu.roll(key_grad[rows:], HD, 1)
            key_grad = (key_grad * (1.0 / math.sqrt(HD))).astype(BF16).astype(F32)
            value_grad = value_acc[part]
            value_grad = pltpu.roll(value_grad[:rows], HD, 1) + value_grad[rows:]
            turned = key_grad * cos_all[spot, :] - swap_halves(key_grad) * sin_all[spot, :]
            out_ref[spot, pl.ds(query_width, 128)] = jnp.where(lane < HD, turned, value_grad).astype(BF16)


def attention_backward(info, query, attended, grad, lse, kv, cosine, sine, rows):
    total, query_width = query.shape
    blocks = total // rows
    pairs = query_width // 128
    row_block = pl.BlockSpec((rows, query_width), lambda j, info: (j, 0))
    table_block = pl.BlockSpec((rows, 128), lambda j, info: (j, 0))
    whole = pl.BlockSpec((total, 128), lambda j, info: (0, 0))
    return pl.pallas_call(
        attention_backward_kernel,
        grid_spec=pltpu.PrefetchScalarGridSpec(
            num_scalar_prefetch=1,
            grid=(blocks,),
            in_specs=[
                row_block, row_block, row_block,
                pl.BlockSpec((2 * pairs, rows), lambda j, info: (0, j)),
                whole, table_block, table_block, whole, whole,
            ],
            out_specs=pl.BlockSpec((total, query_width + 128), lambda j, info: (0, 0)),
            scratch_shapes=[
                pltpu.VMEM((blocks, 2 * rows, 128), BF16),
                pltpu.VMEM((blocks, 2 * rows, 128), BF16),
                pltpu.VMEM((blocks, 2 * rows, 128), F32),
                pltpu.VMEM((blocks, 2 * rows, 128), F32),
                pltpu.VMEM((rows, query_width), F32),
                pltpu.VMEM((2 * pairs, rows), F32),
            ],
        ),
        out_shape=jax.ShapeDtypeStruct((total, query_width + 128), BF16),
        name="attention_backward",
    )(info, query, attended, grad, lse, kv, cosine, sine, cosine, sine)


def norm_scale(values):
    return lax.rsqrt(jnp.mean(values * values, axis=-1, keepdims=True) + EPS)


def norm_backward(values, scale, gain, grads):
    weighted = grads * gain
    gain_grad = jnp.sum(grads * values * scale, axis=0)
    cubed = scale * scale * scale
    value_grad = scale * weighted - values * cubed * jnp.mean(weighted * values, axis=-1, keepdims=True)
    return gain_grad, value_grad


def over_batch(term):
    return lax.psum_scatter(term.astype(BF16), "batch", scatter_dimension=0, tiled=True).astype(F32)


def shards(
    tokens, seq_count, query_weight, key_weight, value_weight, out_weight,
    gate_weight, up_weight, down_weight, attention_gain, feedforward_gain, cotangent,
):
    seq_parts = lax.axis_size("seq")
    batch_parts = lax.axis_size("batch")
    part = lax.axis_index("seq")
    parity = lax.axis_index("batch") % 2
    rows = tokens.shape[1]
    group_rows = rows * seq_parts
    width = tokens.shape[2]

    order = jnp.arange(seq_parts, dtype=jnp.int32)
    swapped = ((order & 1) << 1) | (order >> 1)
    masks = jnp.where(parity == 0, order, swapped)
    owners = part ^ masks
    other = part ^ order
    spots = jnp.where(parity == 0, other, ((other & 1) << 1) | (other >> 1))
    seq_length = group_rows // seq_count[0]
    firsts = (owners * rows) // seq_length * seq_length // rows
    info = jnp.concatenate([owners, spots, firsts]).astype(jnp.int32)

    index = (owners[:, None] * rows + jnp.arange(rows, dtype=jnp.int32)[None, :]).reshape(-1)
    places = index - index // seq_length * seq_length
    lane = jnp.arange(128, dtype=jnp.int32)
    inverse = jnp.exp((lane % (HD // 2)).astype(F32) * (-2.0 * math.log(10000.0) / HD))
    angles = places.astype(F32)[:, None] * inverse[None, :]
    cosine = jnp.cos(angles)
    sine = jnp.sin(angles) * jnp.where(lane % HD < HD // 2, -1.0, 1.0)[None, :]

    inputs = tokens[0].astype(F32)
    scale_one = norm_scale(inputs)
    normed_one = (inputs * scale_one * attention_gain).astype(BF16)
    qkv_weight = jnp.concatenate([query_weight, key_weight, value_weight], axis=1)
    normed_one_blocks = gather_blocks(normed_one)
    qkv = jnp.concatenate([mm(block, qkv_weight) for block in normed_one_blocks], axis=0)
    cotangent_blocks = gather_blocks(cotangent[0])

    attended, query, kv, lse = attention_forward(info, qkv, cosine, sine, rows)
    half = group_rows // 2
    branch_upper = mm(attended[half:], out_weight).astype(BF16)
    branch_lower = mm(attended[:half], out_weight).astype(BF16)
    hidden = inputs + scatter_sum(branch_upper, branch_lower)

    grad_rows = jnp.concatenate(cotangent_blocks, axis=0)
    grad_mixed = mm_nt(grad_rows, down_weight)

    scale_two = norm_scale(hidden)
    normed_two = (hidden * scale_two * feedforward_gain).astype(BF16)
    normed_two_rows = jnp.concatenate(gather_blocks(normed_two), axis=0)
    gate = mm(normed_two_rows, gate_weight)
    upward = mm(normed_two_rows, up_weight)
    sigmoid_gate = jax.nn.sigmoid(gate)
    activated = gate * sigmoid_gate
    mixed = (activated * upward).astype(BF16)
    grad_gate = (grad_mixed * upward * sigmoid_gate * (1.0 + gate * (1.0 - sigmoid_gate))).astype(BF16)
    grad_upward = (grad_mixed * activated).astype(BF16)

    def back_rows(first, last):
        return (
            mm_nt(grad_gate[first:last], gate_weight) + mm_nt(grad_upward[first:last], up_weight)
        ).astype(BF16)

    grad_normed_two = scatter_sum(back_rows(half, group_rows), back_rows(0, half))
    down_grad = over_batch(mm_tn(mixed, grad_rows))
    gate_grad = over_batch(mm_tn(normed_two_rows, grad_gate))
    up_grad = over_batch(mm_tn(normed_two_rows, grad_upward))

    grad_out = cotangent[0].astype(F32)
    feed_gain_term, grad_hidden_norm = norm_backward(hidden, scale_two, feedforward_gain, grad_normed_two)
    grad_hidden = grad_out + grad_hidden_norm
    grad_branch_blocks = gather_blocks(grad_hidden.astype(BF16))
    grad_branch_rows = jnp.concatenate(grad_branch_blocks, axis=0)
    grad_attended = mm_nt(grad_branch_rows, out_weight).astype(BF16)
    out_grad = over_batch(mm_tn(attended, grad_branch_rows))

    ffn_upper = mm(mixed[half:], down_weight).astype(BF16)
    ffn_lower = mm(mixed[:half], down_weight).astype(BF16)
    layer_out = (hidden + scatter_sum(ffn_upper, ffn_lower)).astype(BF16)

    grad_qkv = attention_backward(info, query, attended, grad_attended, lse, kv, cosine, sine, rows)
    normed_one_rows = jnp.concatenate(normed_one_blocks, axis=0)
    grad_normed_one = scatter_sum(
        mm_nt(grad_qkv[half:], qkv_weight).astype(BF16), mm_nt(grad_qkv[:half], qkv_weight).astype(BF16)
    )
    qkv_grad = over_batch(mm_tn(normed_one_rows, grad_qkv))
    attention_gain_term, grad_inputs_norm = norm_backward(inputs, scale_one, attention_gain, grad_normed_one)
    input_grad = grad_hidden + grad_inputs_norm

    devices = seq_parts * batch_parts
    gains = jnp.concatenate(
        [attention_gain_term.reshape(devices, -1), feed_gain_term.reshape(devices, -1)], axis=1
    )
    gains = jnp.sum(lax.all_to_all(gains, ("seq", "batch"), 0, 0, tiled=True), axis=0)
    share = width // devices
    query_width = query_weight.shape[1]
    key_width = key_weight.shape[1]
    return (
        layer_out[None],
        input_grad[None],
        qkv_grad[:, :query_width],
        qkv_grad[:, query_width : query_width + key_width],
        qkv_grad[:, query_width + key_width :],
        out_grad,
        gate_grad,
        up_grad,
        down_grad,
        gains[:share],
        gains[share:],
    )


def solution(mesh):
    return jax.shard_map(
        shards,
        mesh=mesh,
        in_specs=(
            P("batch", "seq", None),
            P("batch"),
            P(None, "seq"),
            P(None, "seq"),
            P(None, "seq"),
            P("seq", None),
            P(None, "seq"),
            P(None, "seq"),
            P("seq", None),
            P(),
            P(),
            P("batch", "seq", None),
        ),
        out_specs=(
            P("batch", "seq", None),
            P("batch", "seq", None),
            P("batch", "seq"),
            P("batch", "seq"),
            P("batch", "seq"),
            P(("seq", "batch"), None),
            P("batch", "seq"),
            P("batch", "seq"),
            P(("seq", "batch"), None),
            P(("seq", "batch")),
            P(("seq", "batch")),
        ),
        check_vma=False,
    )
```

time: 1030 us -> 680 us (0.66)
  waiting for transfers between devices: 684 us -> 374 us
  matrix products: 206 us -> 142 us
  Pallas kernels: 0 us -> 54.4 us
  blocking collectives: 39.5 us -> 0 us
  starting transfers between devices: 0.87 us -> 32.6 us
  other arithmetic: 68.6 us -> 37.8 us
    reduce_scatter x11 -> x5, waiting for transfers between devices: 527 us -> 124 us  [over_batch(): lax.psum_scatter(term.astype(BF16), 'batch', scatter_dimension=0, tiled=T...]
    ppermute x0 -> x20, waiting for transfers between devices: none -> 247 us  [exchange(): return lax.ppermute(values, ('seq', 'batch'), pairs)]
    all_gather x4 -> x0, waiting for transfers between devices: 156 us -> none  [the longest x1 53.2 us: shards(): normed_rows = lax.all_gather(normed_one, 'seq', axis=0, tiled=True)]
    dot_general x33 -> x23, matrix products: 206 us -> 142 us  [the longest x8 51.3 us: mm_nt(): lax.dot_general(a, b, (((1,), (1,)), ((), ())), preferred_element_type=F32)]
    pallas_call x0 -> x2, Pallas kernels: none -> 54.4 us  [the longest x1 27.8 us: attention_forward(): pl.pallas_call(attention_forward_kernel, grid_spec=pltpu.PrefetchScalarGr...]
    unnamed x1 -> x0, blocking collectives: 39.5 us -> none
    ppermute x0 -> x20, starting transfers between devices: none -> 29.6 us  [exchange(): return lax.ppermute(values, ('seq', 'batch'), pairs)]
    another operation x6 -> x0, other arithmetic: 21.3 us -> none
  transfers between devices with their start and end apart: 15 -> 26, of which waited for: 14 -> 17; matrix products, arithmetic and copies ran while one was open for 17% -> 20% of each run, Pallas kernels for 0% -> 4%
where the time goes in v1:
time: 680 us; the launch traced here: 669 us
  waiting for transfers between devices  374 us (55%)
  matrix products  142 us (21%)
  Pallas kernels  54.4 us (8%)
  other arithmetic  37.8 us (6%)
  starting transfers between devices  32.6 us (5%)
  between operations  15.3 us (2%)
  local copies, waits for them, and re-layouts  12.6 us (2%)
    ppermute x20, waiting for transfers between devices, exchange(): return lax.ppermute(values, ('seq', 'batch'), pairs)  247 us
    reduce_scatter x5, waiting for transfers between devices, over_batch(): lax.psum_scatter(term.astype(BF16), 'batch', scatter_dimension=0, tiled=T...  124 us
    dot_general x8, matrix products, mm_nt(): lax.dot_general(a, b, (((1,), (1,)), ((), ())), preferred_element_type=F32)  51.3 us
    dot_general x10, matrix products, mm(): lax.dot_general(a, b, (((1,), (0,)), ((), ())), preferred_element_type=F32)  47 us
    dot_general x5, matrix products, mm_tn(): lax.dot_general(a, b, (((0,), (0,)), ((), ())), preferred_element_type=F32)  44 us
    ppermute x20, starting transfers between devices, exchange(): return lax.ppermute(values, ('seq', 'batch'), pairs)  29.6 us
    pallas_call x1, Pallas kernels, attention_forward(): pl.pallas_call(attention_forward_kernel, grid_spec=pltpu.PrefetchScalarGr...  27.8 us
    pallas_call x1, Pallas kernels, attention_backward(): pl.pallas_call(attention_backward_kernel, grid_spec=pltpu.PrefetchScalarG...  26.6 us
  transfers between devices with their start and end apart: 26, of which 17 were waited for; matrix products, arithmetic and copies ran while one was open for 20% of the time, Pallas kernels for 4%

profile of v1, /device:TPU:0, one launch (start us, length us, event | category | flops | bytes accessed | tf_op | source)
XLA Modules:
  0.0 668.9 jit_solution(9198214624568874034)
XLA Ops:
  9.5 2.5 fusion.14
  12.0 3.0 collective-permute-start.1
  20.1 3.3 fusion.34
  23.5 15.0 %collective-permute-done = bf16[256,2048]{1,0:T(8,128)(2,1)} collective-permute-done((bf16[256,2048]{1,0:T(8,128)(2,1)}, bf16[256,2048]{1,0:T(8,128)(2,1)}, u32[]{:S(2)}, u32[]{:S(2)}) %collective-permute-start) | collective-permute-done | bytes 1048608 | tf_op jit(solution)/shard_map/ppermute | solution.py:37
  47.4 6.0 collective-permute-done.2
  57.1 27.8 %attention_forward.1 = (bf16[1024,512]{1,0:T(8,128)(2,1)}, bf16[1024,512]{1,0:T(8,128)(2,1)}, bf16[1024,128]{1,0:T(8,128)(2,1)}, f32[8,1024]{1,0:T(8,128)}) custom-call(s32[12]{0:T(128)} %pad_add_fusion.info, f32[1024,640]{1,0:T(8,128)} %pad_maximum_fusion.4.query_ref.kv_ref, f32[1024,640]{1,0:T(8,128)} %pad_maximum_fusion.4.query_ref.kv_ref, ...), custom_call_target="tpu_custom_call" | custom-call | tf_op jit(solution)/shard_map/attention_forward/pallas_call | solution.py:174
  84.9 2.4 convolution_convert_fusion.4
  90.4 30.0 %collective-permute-done.3 = bf16[512,2048]{1,0:T(8,128)(2,1)S(1)} collective-permute-done((bf16[512,2048]{1,0:T(8,128)(2,1)S(1)}, bf16[512,2048]{1,0:T(8,128)(2,1)S(1)}, u32[]{:S(2)}, u32[]{:S(2)}) %collective-permute-start.3) | collective-permute-done | bytes 2097184 | tf_op jit(solution)/shard_map/ppermute | solution.py:37
  120.8 3.1 collective-permute-start.4
  123.9 18.2 %collective-permute-done.4 = bf16[256,2048]{1,0:T(8,128)(2,1)S(1)} collective-permute-done((bf16[256,2048]{1,0:T(8,128)(2,1)S(1)}, bf16[256,2048]{1,0:T(8,128)(2,1)S(1)}, u32[]{:S(2)}, u32[]{:S(2)}) %collective-permute-start.4) | collective-permute-done | bytes 1048608 | tf_op jit(solution)/shard_map/ppermute | solution.py:37
  144.4 2.5 collective-permute-start.5
  148.6 22.4 %collective-permute-done.5 = bf16[256,2048]{1,0:T(8,128)(2,1)S(1)} collective-permute-done((bf16[256,2048]{1,0:T(8,128)(2,1)S(1)}, bf16[256,2048]{1,0:T(8,128)(2,1)S(1)}, u32[]{:S(2)}, u32[]{:S(2)}) %collective-permute-start.5) | collective-permute-done | bytes 1048608 | tf_op jit(solution)/shard_map/ppermute | solution.py:37
  173.0 20.4 %collective-permute-done.10 = bf16[256,2048]{1,0:T(8,128)(2,1)S(1)} collective-permute-done((bf16[256,2048]{1,0:T(8,128)(2,1)S(1)}, bf16[256,2048]{1,0:T(8,128)(2,1)S(1)}, u32[]{:S(2)}, u32[]{:S(2)}) %collective-permute-start.10) | collective-permute-done | bytes 1048608 | tf_op jit(solution)/shard_map/ppermute | solution.py:37
  194.8 11.3 %fusion.52 = f32[1024,1408]{1,0:T(8,128)} fusion(bf16[2048,1408]{1,0:T(8,128)(2,1)S(1)} %bitcast.59, bf16[256,2048]{1,0:T(8,128)(2,1)S(1)} %collective-permute-done.7, bf16[256,2048]{1,0:T(8,128)(2,1)S(1)} %collective-permute-done.6, bf16[256,2048]{1,0:T(8,128)(2,1)S(1)} %collective-permute-done.5, bf16[256,2048]{1,0:T(8,128)(2,1)S(1)} %multiply_convert_fusion.3), kind=kOutput, calls=%fused_computation.117 | convolution fusion | flops 5922357248 | bytes 15728640 | tf_op jit(solution)/shard_map/dot_general | solution.py:18
  206.1 11.4 %fusion.53 = f32[1024,1408]{1,0:T(8,128)} fusion(bf16[2048,1408]{1,0:T(8,128)(2,1)S(1)} %bitcast.55, bf16[256,2048]{1,0:T(8,128)(2,1)S(1)} %collective-permute-done.7, bf16[256,2048]{1,0:T(8,128)(2,1)S(1)} %collective-permute-done.6, bf16[256,2048]{1,0:T(8,128)(2,1)S(1)} %collective-permute-done.5, bf16[256,2048]{1,0:T(8,128)(2,1)S(1)} %multiply_convert_fusion.3), kind=kOutput, calls=%fused_computation.118 | convolution fusion | flops 5922357248 | bytes 15728640 | tf_op jit(solution)/shard_map/dot_general | solution.py:18
  218.5 17.0 %multiply_convert_fusion = (bf16[1024,1408]{1,0:T(8,128)(2,1)}, bf16[1024,1408]{1,0:T(8,128)(2,1)}, bf16[1024,1408]{1,0:T(8,128)(2,1)}) fusion(f32[1024,1408]{1,0:T(8,128)} %fusion.53, f32[1024,1408]{1,0:T(8,128)} %fusion.52, bf16[1408,2048]{1,0:T(8,128)(2,1)} %param.20, bf16[256,2048]{1,0:T(8,128)(2,1)} %collective-permute-done.12, ...), kind=kOutput, calls=%fused_computation.3 | convolution fusion | flops 5943984128 | bytes 30146560 | tf_op jit(solution)/shard_map/dot_general | solution.py:22
  235.5 6.1 fusion.23
  241.6 6.5 add_convert_fusion
  248.9 6.6 convolution_convert_fusion.8
  256.9 5.1 fusion.26
  261.9 5.7 add_convert_fusion.1
  267.6 18.2 %collective-permute-done.13 = bf16[512,2048]{1,0:T(8,128)(2,1)S(1)} collective-permute-done((bf16[512,2048]{1,0:T(8,128)(2,1)S(1)}, bf16[512,2048]{1,0:T(8,128)(2,1)S(1)}, u32[]{:S(2)}, u32[]{:S(2)}) %collective-permute-start.13) | collective-permute-done | bytes 2097184 | tf_op jit(solution)/shard_map/ppermute | solution.py:37
  286.2 2.4 collective-permute-start.14
  288.6 6.4 convolution_convert_fusion.9
  295.1 30.0 %collective-permute-done.8 = bf16[512,2048]{1,0:T(8,128)(2,1)S(1)} collective-permute-done((bf16[512,2048]{1,0:T(8,128)(2,1)S(1)}, bf16[512,2048]{1,0:T(8,128)(2,1)S(1)}, u32[]{:S(2)}, u32[]{:S(2)}) %collective-permute-start.8) | collective-permute-done | bytes 2097184 | tf_op jit(solution)/shard_map/ppermute | solution.py:37
  325.5 2.4 collective-permute-start.9
  328.9 19.1 %collective-permute-done.9 = bf16[256,2048]{1,0:T(8,128)(2,1)S(1)} collective-permute-done((bf16[256,2048]{1,0:T(8,128)(2,1)S(1)}, bf16[256,2048]{1,0:T(8,128)(2,1)S(1)}, u32[]{:S(2)}, u32[]{:S(2)}) %collective-permute-start.9) | collective-permute-done | bytes 1048608 | tf_op jit(solution)/shard_map/ppermute | solution.py:37
  348.0 3.0 fusion.54
  353.3 12.8 %collective-permute-done.15 = bf16[256,2048]{1,0:T(8,128)(2,1)S(1)} collective-permute-done((bf16[256,2048]{1,0:T(8,128)(2,1)S(1)}, bf16[256,2048]{1,0:T(8,128)(2,1)S(1)}, u32[]{:S(2)}, u32[]{:S(2)}) %collective-permute-start.15) | collective-permute-done | bytes 1048608 | tf_op jit(solution)/shard_map/ppermute | solution.py:37
  368.1 12.8 %collective-permute-done.17 = bf16[256,2048]{1,0:T(8,128)(2,1)S(1)} collective-permute-done((bf16[256,2048]{1,0:T(8,128)(2,1)S(1)}, bf16[256,2048]{1,0:T(8,128)(2,1)S(1)}, u32[]{:S(2)}, u32[]{:S(2)}) %collective-permute-start.17) | collective-permute-done | bytes 1048608 | tf_op jit(solution)/shard_map/ppermute | solution.py:37
  381.9 3.6 convolution_convert_fusion.3
  385.5 5.5 convolution_convert_fusion.10.grad_ref
  391.0 26.6 %attention_backward.1 = bf16[1024,640]{1,0:T(8,128)(2,1)} custom-call(s32[12]{0:T(128)} %pad_add_fusion.info, bf16[1024,512]{1,0:T(8,128)(2,1)} %get-tuple-element.16.query_ref, bf16[1024,512]{1,0:T(8,128)(2,1)} %get-tuple-element.15.att_ref, bf16[1024,512]{1,0:T(8,128)(2,1)} %convolution_convert_fusion.10.grad_ref, f32[8,1024]{1,0:T(8,128)} %get-tuple-element.17.lse_ref, ...), custom_call_target="tpu_custom_call" | custom-call | tf_op jit(solution)/shard_map/attention_backward/pallas_call | solution.py:307
  417.6 7.7 %fusion.9 = bf16[2048,640]{1,0:T(8,128)(2,1)} fusion(bf16[1024,640]{1,0:T(8,128)(2,1)} %attention_backward.1, bf16[256,2048]{1,0:T(8,128)(2,1)} %copy-done.22, bf16[256,2048]{1,0:T(8,128)(2,1)} %collective-permute-done.1, bf16[256,2048]{1,0:T(8,128)(2,1)} %collective-permute-done, bf16[256,2048]{1,0:T(8,128)(2,1)} %fusion.14), kind=kOutput, calls=%fused_computation.27 | convolution fusion | flops 2702442496 | bytes 8126464 | tf_op jit(solution)/shard_map/dot_general | solution.py:26
  425.4 10.7 %convolution_convert_fusion = bf16[1408,2048]{1,0:T(8,128)(2,1)} fusion(bf16[1024,1408]{1,0:T(8,128)(2,1)} %get-tuple-element.53, bf16[256,2048]{1,0:T(8,128)(2,1)} %collective-permute-done.12, bf16[256,2048]{1,0:T(8,128)(2,1)} %copy-done.27, bf16[256,2048]{1,0:T(8,128)(2,1)} %copy-done.26, bf16[256,2048]{1,0:T(8,128)(2,1)} %bitcast.50), kind=kOutput, calls=%fused_computation | convolution fusion | flops 5925240832 | bytes 12845056 | tf_op jit(solution)/shard_map/dot_general | solution.py:26
  436.2 10.9 %convolution_convert_fusion.1 = bf16[2048,1408]{1,0:T(8,128)(2,1)} fusion(bf16[1024,1408]{1,0:T(8,128)(2,1)} %get-tuple-element.51, bf16[256,2048]{1,0:T(8,128)(2,1)} %copy-done.25, bf16[256,2048]{1,0:T(8,128)(2,1)} %copy-done.24, bf16[256,2048]{1,0:T(8,128)(2,1)} %copy-done.23, bf16[256,2048]{1,0:T(8,128)(2,1)S(1)} %multiply_convert_fusion.3), kind=kOutput, calls=%fused_computation.1 | convolution fusion | flops 5925240832 | bytes 12845056 | tf_op jit(solution)/shard_map/dot_general | solution.py:26
  447.2 11.1 %convolution_convert_fusion.2 = bf16[2048,1408]{1,0:T(8,128)(2,1)} fusion(bf16[1024,1408]{1,0:T(8,128)(2,1)} %get-tuple-element.52, bf16[256,2048]{1,0:T(8,128)(2,1)} %copy-done.25, bf16[256,2048]{1,0:T(8,128)(2,1)} %copy-done.24, bf16[256,2048]{1,0:T(8,128)(2,1)} %copy-done.23, bf16[256,2048]{1,0:T(8,128)(2,1)S(1)} %multiply_convert_fusion.3), kind=kOutput, calls=%fused_computation.2 | convolution fusion | flops 5925240832 | bytes 12845056 | tf_op jit(solution)/shard_map/dot_general | solution.py:26
  459.6 3.7 convolution_convert_fusion.6
  465.3 27.2 %collective-permute-done.18 = bf16[512,2048]{1,0:T(8,128)(2,1)S(1)} collective-permute-done((bf16[512,2048]{1,0:T(8,128)(2,1)S(1)}, bf16[512,2048]{1,0:T(8,128)(2,1)S(1)}, u32[]{:S(2)}, u32[]{:S(2)}) %collective-permute-start.18) | collective-permute-done | bytes 2097184 | tf_op jit(solution)/shard_map/ppermute | solution.py:37
  497.0 13.3 %collective-permute-done.19 = bf16[256,2048]{1,0:T(8,128)(2,1)} collective-permute-done((bf16[256,2048]{1,0:T(8,128)(2,1)}, bf16[256,2048]{1,0:T(8,128)(2,1)}, u32[]{:S(2)}, u32[]{:S(2)}) %collective-permute-start.19) | collective-permute-done | bytes 1048608 | tf_op jit(solution)/shard_map/ppermute | solution.py:37
  510.3 3.3 fusion.21
  514.4 2.8 all-to-all-start
  517.2 4.7 fusion.18
  521.9 2.6 all-to-all-done
  531.2 2.4 convert_element_type.227
  533.6 60.9 %reduce-scatter.12.cloned.1.call-done = bf16[256,1408]{1,0:T(8,128)(2,1)} async-done(((bf16[2048,1408]{1,0:T(8,128)(2,1)}), bf16[256,1408]{1,0:T(8,128)(2,1)}) %reduce-scatter.12.cloned.1.call-update) | async-done | bytes 720912 | tf_op jit(solution)/shard_map/reduce_scatter | solution.py:345
  594.4 2.3 convert_element_type.225
  596.7 63.1 %reduce-scatter.10.cloned.1.call-done = bf16[256,1408]{1,0:T(8,128)(2,1)} async-done(((bf16[2048,1408]{1,0:T(8,128)(2,1)}), bf16[256,1408]{1,0:T(8,128)(2,1)}) %reduce-scatter.10.cloned.1.call-update) | async-done | bytes 720912 | tf_op jit(solution)/shard_map/reduce_scatter | solution.py:345
  (163 shorter events, 58.0 us)
Async XLA Ops:
  7.2 77.7 %copy-start = (bf16[512,2048]{1,0:T(8,128)(2,1)S(1)}, bf16[512,2048]{1,0:T(8,128)(2,1)}, u32[]{:S(2)}) copy-start(bf16[512,2048]{1,0:T(8,128)(2,1)} %param.17) | copy-start | bytes 6291460
  7.2 518.0 %reduce-scatter.8.cloned.1.call-start = ((), (), s32[]{:S(2)}) async-start(), calls=%async_computation.7 | async-start | bytes 2359296 | tf_op jit(solution)/shard_map/reduce_scatter | solution.py:345
  12.0 33.2 %collective-permute-start.1 = (bf16[256,2048]{1,0:T(8,128)(2,1)}, bf16[256,2048]{1,0:T(8,128)(2,1)}, u32[]{:S(2)}, u32[]{:S(2)}) collective-permute-start(bf16[256,2048]{1,0:T(8,128)(2,1)} %fusion.14), channel_id=1, source_target_pairs={{0,16},{1,9},{2,18},{3,11},{4,20},{5,13},{6,22},{7,15},{8,24},{9,1... | collective-permute-start | bytes 3145736 | tf_op jit(solution)/shard_map/ppermute | solution.py:37
  15.0 23.4 %collective-permute-start = (bf16[256,2048]{1,0:T(8,128)(2,1)}, bf16[256,2048]{1,0:T(8,128)(2,1)}, u32[]{:S(2)}, u32[]{:S(2)}) collective-permute-start(bf16[256,2048]{1,0:T(8,128)(2,1)} %fusion.14), channel_id=1, source_target_pairs={{0,8},{1,17},{2,10},{3,19},{4,12},{5,21},{6,14},{7,23},{8,0},{9,25... | collective-permute-start | bytes 3145736 | tf_op jit(solution)/shard_map/ppermute | solution.py:37
  20.1 33.4 %copy-start.7 = (bf16[2048,640]{1,0:T(8,128)(2,1)}, bf16[2048,640]{1,0:T(8,128)(2,1)S(1)}, u32[]{:S(2)}) copy-start(bf16[2048,640]{1,0:T(8,128)(2,1)S(1)} %pad_maximum_fusion.3) | copy-start | bytes 7864324
  38.4 15.0 %collective-permute-start.2 = (bf16[256,2048]{1,0:T(8,128)(2,1)}, bf16[256,2048]{1,0:T(8,128)(2,1)S(1)}, u32[]{:S(2)}, u32[]{:S(2)}) collective-permute-start(bf16[256,2048]{1,0:T(8,128)(2,1)} %collective-permute-done), channel_id=1, source_target_pairs={{0,16},{1,9},{2,18},{3,11},{4,20},{5,13},{6,22},{7,15},{8,24},{9,1... | collective-permute-start | bytes 3145736 | tf_op jit(solution)/shard_map/ppermute | solution.py:37
  87.3 33.1 %collective-permute-start.3 = (bf16[512,2048]{1,0:T(8,128)(2,1)S(1)}, bf16[512,2048]{1,0:T(8,128)(2,1)S(1)}, u32[]{:S(2)}, u32[]{:S(2)}) collective-permute-start(bf16[512,2048]{1,0:T(8,128)(2,1)S(1)} %convolution_convert_fusion.4), channel_id=1, source_target_pairs={{0,16},{1,9},{2,18},{3,11},{4,20},{5,13},{6,22},{7,15},{8,24},{9,1... | collective-permute-start | bytes 6291464 | tf_op jit(solution)/shard_map/ppermute | solution.py:37
  90.4 51.7 %copy-start.3 = (bf16[1,256,2048]{2,1,0:T(8,128)(2,1)S(1)}, bf16[1,256,2048]{2,1,0:T(8,128)(2,1)}, u32[]{:S(2)}) copy-start(bf16[1,256,2048]{2,1,0:T(8,128)(2,1)} %param.12) | copy-start | bytes 3145732
  120.4 74.4 %slice-start.4 = ((s8[5767168]{0:T(1024)(128)(4,1)}), s8[4194304]{0:T(1024)(128)(4,1)S(1)}, s32[]{:S(2)}) async-start(s8[5767168]{0:T(1024)(128)(4,1)} %bitcast.58), calls=%async_computation.15 | async-start | bytes 8388608
  120.8 23.4 %copy-start.17 = (f32[2048]{0:T(1024)S(1)}, f32[2048]{0:T(1024)}, u32[]{:S(2)}) copy-start(f32[2048]{0:T(1024)} %param.22) | copy-start | bytes 24580
  120.8 74.0 %slice-start.5 = ((s8[5767168]{0:T(1024)(128)(4,1)}), s8[1572864]{0:T(1024)(128)(4,1)S(1)}, s32[]{:S(2)}) async-start(s8[5767168]{0:T(1024)(128)(4,1)} %bitcast.58), calls=%async_computation.16 | async-start | bytes 3145728
  120.8 21.3 %collective-permute-start.4 = (bf16[256,2048]{1,0:T(8,128)(2,1)S(1)}, bf16[256,2048]{1,0:T(8,128)(2,1)S(1)}, u32[]{:S(2)}, u32[]{:S(2)}) collective-permute-start(bf16[256,2048]{1,0:T(8,128)(2,1)S(1)} %add_convert_fusion.6), channel_id=1, source_target_pairs={{0,8},{1,17},{2,10},{3,19},{4,12},{5,21},{6,14},{7,23},{8,0},{9,25... | collective-permute-start | bytes 3145736 | tf_op jit(solution)/shard_map/ppermute | solution.py:37
  144.4 26.6 %collective-permute-start.5 = (bf16[256,2048]{1,0:T(8,128)(2,1)S(1)}, bf16[256,2048]{1,0:T(8,128)(2,1)S(1)}, u32[]{:S(2)}, u32[]{:S(2)}) collective-permute-start(bf16[256,2048]{1,0:T(8,128)(2,1)S(1)} %multiply_convert_fusion.3), channel_id=1, source_target_pairs={{0,8},{1,17},{2,10},{3,19},{4,12},{5,21},{6,14},{7,23},{8,0},{9,25... | collective-permute-start | bytes 3145736 | tf_op jit(solution)/shard_map/ppermute | solution.py:37
  147.0 59.1 %slice-start = ((s8[5767168]{0:T(1024)(128)(4,1)}), s8[4194304]{0:T(1024)(128)(4,1)S(1)}, s32[]{:S(2)}) async-start(s8[5767168]{0:T(1024)(128)(4,1)} %bitcast.54), calls=%async_computation.11 | async-start | bytes 8388608
  147.0 59.1 %slice-start.1 = ((s8[5767168]{0:T(1024)(128)(4,1)}), s8[1572864]{0:T(1024)(128)(4,1)S(1)}, s32[]{:S(2)}) async-start(s8[5767168]{0:T(1024)(128)(4,1)} %bitcast.54), calls=%async_computation.12 | async-start | bytes 3145728
  147.0 46.5 %collective-permute-start.10 = (bf16[256,2048]{1,0:T(8,128)(2,1)S(1)}, bf16[256,2048]{1,0:T(8,128)(2,1)S(1)}, u32[]{:S(2)}, u32[]{:S(2)}) collective-permute-start(bf16[256,2048]{1,0:T(8,128)(2,1)S(1)} %bitcast.51), channel_id=1, source_target_pairs={{0,8},{1,17},{2,10},{3,19},{4,12},{5,21},{6,14},{7,23},{8,0},{9,25... | collective-permute-start | bytes 3145736 | tf_op jit(solution)/shard_map/ppermute | solution.py:37
  147.3 47.4 %collective-permute-start.6 = (bf16[256,2048]{1,0:T(8,128)(2,1)S(1)}, bf16[256,2048]{1,0:T(8,128)(2,1)S(1)}, u32[]{:S(2)}, u32[]{:S(2)}) collective-permute-start(bf16[256,2048]{1,0:T(8,128)(2,1)S(1)} %multiply_convert_fusion.3), channel_id=1, source_target_pairs={{0,16},{1,9},{2,18},{3,11},{4,20},{5,13},{6,22},{7,15},{8,24},{9,1... | collective-permute-start | bytes 3145736 | tf_op jit(solution)/shard_map/ppermute | solution.py:37
  171.0 35.1 %copy-start.23 = (bf16[256,2048]{1,0:T(8,128)(2,1)}, bf16[256,2048]{1,0:T(8,128)(2,1)S(1)}, u32[]{:S(2)}) copy-start(bf16[256,2048]{1,0:T(8,128)(2,1)S(1)} %collective-permute-done.5) | copy-start | bytes 3145732
  171.0 23.7 %collective-permute-start.7 = (bf16[256,2048]{1,0:T(8,128)(2,1)S(1)}, bf16[256,2048]{1,0:T(8,128)(2,1)S(1)}, u32[]{:S(2)}, u32[]{:S(2)}) collective-permute-start(bf16[256,2048]{1,0:T(8,128)(2,1)S(1)} %collective-permute-done.5), channel_id=1, source_target_pairs={{0,16},{1,9},{2,18},{3,11},{4,20},{5,13},{6,22},{7,15},{8,24},{9,1... | collective-permute-start | bytes 3145736 | tf_op jit(solution)/shard_map/ppermute | solution.py:37
  172.2 45.2 %collective-permute-start.11 = (bf16[256,2048]{1,0:T(8,128)(2,1)S(1)}, bf16[256,2048]{1,0:T(8,128)(2,1)S(1)}, u32[]{:S(2)}, u32[]{:S(2)}) collective-permute-start(bf16[256,2048]{1,0:T(8,128)(2,1)S(1)} %bitcast.52), channel_id=1, source_target_pairs={{0,16},{1,9},{2,18},{3,11},{4,20},{5,13},{6,22},{7,15},{8,24},{9,1... | collective-permute-start | bytes 3145736 | tf_op jit(solution)/shard_map/ppermute | solution.py:37
  193.5 25.0 %collective-permute-start.12 = (bf16[256,2048]{1,0:T(8,128)(2,1)S(1)}, bf16[256,2048]{1,0:T(8,128)(2,1)}, u32[]{:S(2)}, u32[]{:S(2)}) collective-permute-start(bf16[256,2048]{1,0:T(8,128)(2,1)S(1)} %collective-permute-done.10), channel_id=1, source_target_pairs={{0,16},{1,9},{2,18},{3,11},{4,20},{5,13},{6,22},{7,15},{8,24},{9,1... | collective-permute-start | bytes 3145736 | tf_op jit(solution)/shard_map/ppermute | solution.py:37
  241.6 15.3 %slice-start.2 = ((s8[5767168]{0:T(1024)(128)(4,1)}), s8[4194304]{0:T(1024)(128)(4,1)S(1)}, s32[]{:S(2)}) async-start(s8[5767168]{0:T(1024)(128)(4,1)} %bitcast.56), calls=%async_computation.13 | async-start | bytes 8388608
  241.6 20.4 %slice-start.6 = ((s8[5767168]{0:T(1024)(128)(4,1)}), s8[4194304]{0:T(1024)(128)(4,1)S(1)}, s32[]{:S(2)}) async-start(s8[5767168]{0:T(1024)(128)(4,1)} %bitcast.60), calls=%async_computation.17 | async-start | bytes 8388608
  248.1 37.8 %collective-permute-start.13 = (bf16[512,2048]{1,0:T(8,128)(2,1)S(1)}, bf16[512,2048]{1,0:T(8,128)(2,1)S(1)}, u32[]{:S(2)}, u32[]{:S(2)}) collective-permute-start(bf16[512,2048]{1,0:T(8,128)(2,1)S(1)} %add_convert_fusion), channel_id=1, source_target_pairs={{0,16},{1,9},{2,18},{3,11},{4,20},{5,13},{6,22},{7,15},{8,24},{9,1... | collective-permute-start | bytes 6291464 | tf_op jit(solution)/shard_map/ppermute | solution.py:37
  255.6 69.5 %collective-permute-start.8 = (bf16[512,2048]{1,0:T(8,128)(2,1)S(1)}, bf16[512,2048]{1,0:T(8,128)(2,1)S(1)}, u32[]{:S(2)}, u32[]{:S(2)}) collective-permute-start(bf16[512,2048]{1,0:T(8,128)(2,1)S(1)} %convolution_convert_fusion.8), channel_id=1, source_target_pairs={{0,16},{1,9},{2,18},{3,11},{4,20},{5,13},{6,22},{7,15},{8,24},{9,1... | collective-permute-start | bytes 6291464 | tf_op jit(solution)/shard_map/ppermute | solution.py:37
  267.6 21.0 %copy-start.33 = (bf16[1024,1408]{1,0:T(8,128)(2,1)S(1)}, bf16[1024,1408]{1,0:T(8,128)(2,1)}, u32[]{:S(2)}) copy-start(bf16[1024,1408]{1,0:T(8,128)(2,1)} %get-tuple-element.53) | copy-start | bytes 8650756
  286.2 41.6 %collective-permute-start.14 = (bf16[256,2048]{1,0:T(8,128)(2,1)S(1)}, bf16[256,2048]{1,0:T(8,128)(2,1)S(1)}, u32[]{:S(2)}, u32[]{:S(2)}) collective-permute-start(bf16[256,2048]{1,0:T(8,128)(2,1)S(1)} %add_convert_fusion.3), channel_id=1, source_target_pairs={{0,8},{1,17},{2,10},{3,19},{4,12},{5,21},{6,14},{7,23},{8,0},{9,25... | collective-permute-start | bytes 3145736 | tf_op jit(solution)/shard_map/ppermute | solution.py:37
  295.1 32.8 %copy-start.2 = (f32[256,2048]{1,0:T(8,128)S(1)}, f32[256,2048]{1,0:T(8,128)}, u32[]{:S(2)}) copy-start(f32[256,2048]{1,0:T(8,128)} %copy-done.1) | copy-start | bytes 6291460
  325.5 22.5 %copy-start.13 = (bf16[1,256,2048]{2,1,0:T(8,128)(2,1)S(1)}, bf16[1,256,2048]{2,1,0:T(8,128)(2,1)}, u32[]{:S(2)}) copy-start(bf16[1,256,2048]{2,1,0:T(8,128)(2,1)} %param.23) | copy-start | bytes 3145732
  325.5 22.5 %collective-permute-start.9 = (bf16[256,2048]{1,0:T(8,128)(2,1)S(1)}, bf16[256,2048]{1,0:T(8,128)(2,1)S(1)}, u32[]{:S(2)}, u32[]{:S(2)}) collective-permute-start(bf16[256,2048]{1,0:T(8,128)(2,1)S(1)} %add_convert_fusion.5), channel_id=1, source_target_pairs={{0,8},{1,17},{2,10},{3,19},{4,12},{5,21},{6,14},{7,23},{8,0},{9,25... | collective-permute-start | bytes 3145736 | tf_op jit(solution)/shard_map/ppermute | solution.py:37
  348.0 33.9 %copy-start.11 = (bf16[1024,512]{1,0:T(8,128)(2,1)S(1)}, bf16[1024,512]{1,0:T(8,128)(2,1)}, u32[]{:S(2)}) copy-start(bf16[1024,512]{1,0:T(8,128)(2,1)} %get-tuple-element.15.att_ref) | copy-start | bytes 3145732
  351.0 29.9 %copy-start.14 = (bf16[256,2048]{1,0:T(8,128)(2,1)}, bf16[256,2048]{1,0:T(8,128)(2,1)S(1)}, u32[]{:S(2)}) copy-start(bf16[256,2048]{1,0:T(8,128)(2,1)S(1)} %get-tuple-element.45) | copy-start | bytes 3145732
  351.0 15.1 %collective-permute-start.15 = (bf16[256,2048]{1,0:T(8,128)(2,1)S(1)}, bf16[256,2048]{1,0:T(8,128)(2,1)S(1)}, u32[]{:S(2)}, u32[]{:S(2)}) collective-permute-start(bf16[256,2048]{1,0:T(8,128)(2,1)S(1)} %get-tuple-element.45), channel_id=1, source_target_pairs={{0,8},{1,17},{2,10},{3,19},{4,12},{5,21},{6,14},{7,23},{8,0},{9,25... | collective-permute-start | bytes 3145736 | tf_op jit(solution)/shard_map/ppermute | solution.py:37
  353.3 14.8 %collective-permute-start.16 = (bf16[256,2048]{1,0:T(8,128)(2,1)S(1)}, bf16[256,2048]{1,0:T(8,128)(2,1)S(1)}, u32[]{:S(2)}, u32[]{:S(2)}) collective-permute-start(bf16[256,2048]{1,0:T(8,128)(2,1)S(1)} %get-tuple-element.45), channel_id=1, source_target_pairs={{0,16},{1,9},{2,18},{3,11},{4,20},{5,13},{6,22},{7,15},{8,24},{9,1... | collective-permute-start | bytes 3145736 | tf_op jit(solution)/shard_map/ppermute | solution.py:37
  366.1 14.8 %copy-start.28 = (bf16[256,2048]{1,0:T(8,128)(2,1)}, bf16[256,2048]{1,0:T(8,128)(2,1)S(1)}, u32[]{:S(2)}) copy-start(bf16[256,2048]{1,0:T(8,128)(2,1)S(1)} %collective-permute-done.15) | copy-start | bytes 3145732
  366.1 14.8 %collective-permute-start.17 = (bf16[256,2048]{1,0:T(8,128)(2,1)S(1)}, bf16[256,2048]{1,0:T(8,128)(2,1)S(1)}, u32[]{:S(2)}, u32[]{:S(2)}) collective-permute-start(bf16[256,2048]{1,0:T(8,128)(2,1)S(1)} %collective-permute-done.15), channel_id=1, source_target_pairs={{0,16},{1,9},{2,18},{3,11},{4,20},{5,13},{6,22},{7,15},{8,24},{9,1... | collective-permute-start | bytes 3145736 | tf_op jit(solution)/shard_map/ppermute | solution.py:37
  385.5 141.5 %reduce-scatter.6.cloned.1.call-start = ((), (), s32[]{:S(2)}) async-start(), calls=%async_computation.6 | async-start | bytes 2949120 | tf_op jit(solution)/shard_map/reduce_scatter | solution.py:345
  425.3 105.9 %reduce-scatter.14.cloned.1.call-start = ((), (), s32[]{:S(2)}) async-start(), calls=%async_computation.10 | async-start | bytes 6488064 | tf_op jit(solution)/shard_map/reduce_scatter | solution.py:345
  436.1 158.3 %reduce-scatter.12.cloned.1.call-start = ((), (), s32[]{:S(2)}) async-start(), calls=%async_computation.9 | async-start | bytes 6488064 | tf_op jit(solution)/shard_map/reduce_scatter | solution.py:345
  447.1 212.7 %reduce-scatter.10.cloned.1.call-start = ((), (), s32[]{:S(2)}) async-start(), calls=%async_computation.8 | async-start | bytes 6488064 | tf_op jit(solution)/shard_map/reduce_scatter | solution.py:345
  463.3 29.2 %collective-permute-start.18 = (bf16[512,2048]{1,0:T(8,128)(2,1)S(1)}, bf16[512,2048]{1,0:T(8,128)(2,1)S(1)}, u32[]{:S(2)}, u32[]{:S(2)}) collective-permute-start(bf16[512,2048]{1,0:T(8,128)(2,1)S(1)} %convolution_convert_fusion.6), channel_id=1, source_target_pairs={{0,16},{1,9},{2,18},{3,11},{4,20},{5,13},{6,22},{7,15},{8,24},{9,1... | collective-permute-start | bytes 6291464 | tf_op jit(solution)/shard_map/ppermute | solution.py:37
  465.3 29.9 %copy-start.6 = (bf16[512,2048]{1,0:T(8,128)(2,1)}, bf16[512,2048]{1,0:T(8,128)(2,1)S(1)}, u32[]{:S(2)}) copy-start(bf16[512,2048]{1,0:T(8,128)(2,1)S(1)} %convolution_convert_fusion.7) | copy-start | bytes 6291460
  465.3 45.0 %copy-start.4 = (bf16[1,256,2048]{2,1,0:T(8,128)(2,1)S(1)}, bf16[1,256,2048]{2,1,0:T(8,128)(2,1)}, u32[]{:S(2)}) copy-start(bf16[1,256,2048]{2,1,0:T(8,128)(2,1)} %param.12) | copy-start | bytes 3145732
  465.3 45.0 %copy-start.18 = (f32[2048]{0:T(1024)S(1)}, f32[2048]{0:T(1024)}, u32[]{:S(2)}) copy-start(f32[2048]{0:T(1024)} %param.21) | copy-start | bytes 24580
  465.3 45.0 %copy-start.20 = (f32[256]{0:T(256)S(1)}, f32[256]{0:T(256)}, u32[]{:S(2)}) copy-start(f32[256]{0:T(256)} %copy-done.19) | copy-start | bytes 3076
  495.2 22.0 %copy-start.21 = (f32[256]{0:T(256)S(1)}, f32[256]{0:T(256)}, u32[]{:S(2)}) copy-start(f32[256]{0:T(256)} %get-tuple-element.59) | copy-start | bytes 3076
  495.2 15.1 %collective-permute-start.19 = (bf16[256,2048]{1,0:T(8,128)(2,1)}, bf16[256,2048]{1,0:T(8,128)(2,1)}, u32[]{:S(2)}, u32[]{:S(2)}) collective-permute-start(bf16[256,2048]{1,0:T(8,128)(2,1)} %add_convert_fusion.2), channel_id=1, source_target_pairs={{0,8},{1,17},{2,10},{3,19},{4,12},{5,21},{6,14},{7,23},{8,0},{9,25... | collective-permute-start | bytes 3145736 | tf_op jit(solution)/shard_map/ppermute | solution.py:37
  514.4 10.1 %all-to-all-start = ((f32[32,1,128]{2,1,0:T(1,128)}), f32[32,1,128]{2,1,0:T(1,128)S(1)}, u32[]{:S(2)}, u32[]{:S(2)}) async-start(f32[32,1,128]{2,1,0:T(1,128)} %bitcast.7), calls=%async_computation.5 | async-start | bytes 32768 | tf_op jit(solution)/shard_map/all_to_all | solution.py:441
  (20 other events, 130.3 us)
Sparse Core Ops, SparseCore 0:
  385.6 35.2 reduce-scatter.7
  425.5 36.9 reduce-scatter.5
  464.8 64.1 reduce-scatter.13
  531.1 63.2 reduce-scatter.11
  596.6 63.2 reduce-scatter.9

commit v2 on v1

v2 whole, which is shorter than its diff:
```python
import functools
import math

import jax
import jax.numpy as jnp
from jax import lax
from jax.experimental import pallas as pl
from jax.experimental.pallas import tpu as pltpu
from jax.sharding import PartitionSpec as P

HD = 64
EPS = 1e-05
NEG = -1e30
F32 = jnp.float32
BF16 = jnp.bfloat16


def mm(a, b):
    return lax.dot_general(a, b, (((1,), (0,)), ((), ())), preferred_element_type=F32)


def mm_nt(a, b):
    return lax.dot_general(a, b, (((1,), (1,)), ((), ())), preferred_element_type=F32)


def mm_tn(a, b):
    return lax.dot_general(a, b, (((0,), (0,)), ((), ())), preferred_element_type=F32)


def exchange(values, even_mask, odd_mask):
    seq_parts = lax.axis_size("seq")
    batch_parts = lax.axis_size("batch")
    pairs = []
    for part in range(seq_parts):
        for group in range(batch_parts):
            mask = even_mask if group % 2 == 0 else odd_mask
            pairs.append((part * batch_parts + group, (part ^ mask) * batch_parts + group))
    return lax.ppermute(values, ("seq", "batch"), pairs)


def after(value, *others):
    return lax.optimization_barrier((value, *others))[0]


def first_swap(values):
    return exchange(values, 1, 2)


def second_swap(values):
    return exchange(values, 2, 1)


def split_sum(lower, arrived):
    rows = lower.shape[0] // 2
    total = lower.astype(F32) + arrived.astype(F32)
    return total[:rows], total[rows:].astype(BF16)


def swap_halves(values):
    lane = lax.broadcasted_iota(jnp.int32, values.shape, 1)
    ahead = pltpu.roll(values, values.shape[1] - HD // 2, 1)
    behind = pltpu.roll(values, HD // 2, 1)
    return jnp.where(lane % HD < HD // 2, ahead, behind)


def padded_keys(keys_values):
    lane = lax.broadcasted_iota(jnp.int32, keys_values.shape, 1)
    zero = jnp.zeros_like(keys_values)
    left = jnp.where(lane < HD, keys_values, zero)
    right = pltpu.roll(left, HD, 1)
    return jnp.concatenate([left, right], axis=0)


def padded_values(keys_values):
    lane = lax.broadcasted_iota(jnp.int32, keys_values.shape, 1)
    zero = jnp.zeros_like(keys_values)
    right = jnp.where(lane >= HD, keys_values, zero)
    left = pltpu.roll(right, HD, 1)
    return jnp.concatenate([left, right], axis=0)


def attention_forward_kernel(
    first, info, query_ref, kv_ref, cos_ref, sin_ref, cos_all, sin_all,
    attended_ref, rotated_ref, kv_out, lse_ref, keys_s, values_s, acc_s, max_s,
):
    step = pl.program_id(0) + first
    rows = query_ref.shape[0]
    pairs = query_ref.shape[1] // 128
    blocks = kv_ref.shape[0] // rows

    @pl.when(step == first)
    def _():
        for part in range(blocks):
            here = pl.ds(part * rows, rows)
            kv = kv_ref[here, :]
            lane = lax.broadcasted_iota(jnp.int32, kv.shape, 1)
            turned = kv * cos_all[here, :] + swap_halves(kv) * sin_all[here, :]
            kv = jnp.where(lane < HD, turned, kv).astype(BF16).astype(F32)
            kv_out[here, :] = kv.astype(BF16)
            keys_s[part] = (padded_keys(kv) * (1.0 / math.sqrt(HD))).astype(BF16)
            both = jnp.transpose(padded_values(kv))
            feature = lax.broadcasted_iota(jnp.int32, both.shape, 0)
            key = lax.broadcasted_iota(jnp.int32, both.shape, 1)
            ones = jnp.where((feature < HD) == (key < rows), 1.0, 0.0)
            values_s[part] = jnp.concatenate([both, ones], axis=0).astype(BF16)

    own = info[step]
    low = info[2 * blocks + step]
    key_index = lax.broadcasted_iota(jnp.int32, (2 * rows, rows), 0) % rows
    query_index = lax.broadcasted_iota(jnp.int32, (2 * rows, rows), 1)
    allowed = key_index <= query_index
    at = info[blocks + own]

    def spread(upper, lower, height):
        return jnp.concatenate(
            [jnp.broadcast_to(upper, (height, rows)), jnp.broadcast_to(lower, (height, rows))], axis=0
        )

    for pair in range(pairs):
        cols = pl.ds(pair * 128, 128)
        query = query_ref[:, cols]
        query = (query * cos_ref[...] + swap_halves(query) * sin_ref[...]).astype(BF16)
        rotated_ref[:, cols] = query
        scores = jnp.where(allowed, mm_nt(keys_s[at], query), NEG)
        tops = [jnp.max(scores[i * rows : (i + 1) * rows], axis=0, keepdims=True) for i in range(2)]
        probs = jnp.exp(scores - spread(*tops, rows)).astype(BF16)
        for i in range(2):
            max_s[2 * pair + i : 2 * pair + i + 1, :] = tops[i]
        acc_s[pair] = mm(values_s[at], probs)

    for back in range(1, blocks):

        @pl.when(own - back >= low)
        def _():
            there = info[blocks + jnp.maximum(own - back, 0)]
            for pair in range(pairs):
                query = rotated_ref[:, pl.ds(pair * 128, 128)]
                scores = mm_nt(keys_s[there], query)
                tops, scales = [], []
                for i in range(2):
                    before = max_s[2 * pair + i : 2 * pair + i + 1, :]
                    top = jnp.maximum(
                        before, jnp.max(scores[i * rows : (i + 1) * rows], axis=0, keepdims=True)
                    )
                    tops.append(top)
                    scales.append(jnp.exp(before - top))
                    max_s[2 * pair + i : 2 * pair + i + 1, :] = top
                probs = jnp.exp(scores - spread(*tops, rows)).astype(BF16)
                factor = spread(*scales, HD)
                factor = jnp.concatenate([factor, factor], axis=0)
                acc_s[pair] = acc_s[pair] * factor + mm(values_s[there], probs)

    for pair in range(pairs):
        total = acc_s[pair][128:, :]
        result = acc_s[pair][:128, :] / total
        attended_ref[:, pl.ds(pair * 128, 128)] = jnp.transpose(result).astype(BF16)
        for i in range(2):
            spot = slice(2 * pair + i, 2 * pair + i + 1)
            lse_ref[spot, :] = max_s[spot, :] + jnp.log(total[i * HD : i * HD + 1, :])


def attention_forward(info, qkv, cosine, sine, rows, first, count):
    total, width = qkv.shape
    blocks = total // rows
    query_width = width - 2 * HD
    pairs = query_width // 128
    last = query_width // 128
    return pl.pallas_call(
        functools.partial(attention_forward_kernel, first),
        grid_spec=pltpu.PrefetchScalarGridSpec(
            num_scalar_prefetch=1,
            grid=(count,),
            in_specs=[
                pl.BlockSpec((rows, query_width), lambda j, info: (j + first, 0)),
                pl.BlockSpec((total, 128), lambda j, info: (0, last)),
                pl.BlockSpec((rows, 128), lambda j, info: (j + first, 0)),
                pl.BlockSpec((rows, 128), lambda j, info: (j + first, 0)),
                pl.BlockSpec((total, 128), lambda j, info: (0, 0)),
                pl.BlockSpec((total, 128), lambda j, info: (0, 0)),
            ],
            out_specs=[
                pl.BlockSpec((rows, query_width), lambda j, info: (j, 0)),
                pl.BlockSpec((rows, query_width), lambda j, info: (j, 0)),
                pl.BlockSpec((total, 128), lambda j, info: (0, 0)),
                pl.BlockSpec((2 * pairs, rows), lambda j, info: (0, j)),
            ],
            scratch_shapes=[
                pltpu.VMEM((blocks, 2 * rows, 128), BF16),
                pltpu.VMEM((blocks, 256, 2 * rows), BF16),
                pltpu.VMEM((pairs, 256, rows), F32),
                pltpu.VMEM((2 * pairs, rows), F32),
            ],
        ),
        cost_estimate=pl.CostEstimate(flops=count * 4 * 10**9, bytes_accessed=count * 10**6, transcendentals=0),
        out_shape=[
            jax.ShapeDtypeStruct((count * rows, query_width), BF16),
            jax.ShapeDtypeStruct((count * rows, query_width), BF16),
            jax.ShapeDtypeStruct((total, 128), BF16),
            jax.ShapeDtypeStruct((2 * pairs, count * rows), F32),
        ],
        name="attention_forward",
    )(info, qkv, qkv, cosine, sine, cosine, sine)


def attention_backward_kernel(
    first, final, info, query_ref, att_ref, grad_ref, lse_ref, kv_ref, cos_ref, sin_ref, cos_all, sin_all, *refs
):
    if first:
        refs = refs[1:]
        key_in, value_in = refs[:2]
        refs = refs[2:]
    else:
        key_in = value_in = None
    out_ref, key_acc, value_acc = refs[:3]
    refs = refs[3:]
    if final:
        kv_out = refs[0]
        refs = refs[1:]
    keys_s, values_s, query_acc, delta_s = refs
    step = pl.program_id(0) + first
    rows = query_ref.shape[0]
    query_width = query_ref.shape[1]
    pairs = query_width // 128
    blocks = kv_ref.shape[0] // rows

    @pl.when(step == first)
    def _():
        for part in range(blocks):
            kv = kv_ref[pl.ds(part * rows, rows), :].astype(F32)
            keys_s[part] = (padded_keys(kv) * (1.0 / math.sqrt(HD))).astype(BF16)
            values_s[part] = padded_values(kv).astype(BF16)
        if first:
            key_acc[...] = key_in[...]
            value_acc[...] = value_in[...]
        else:
            key_acc[...] = jnp.zeros_like(key_acc)
            value_acc[...] = jnp.zeros_like(value_acc)

    own = info[step]
    low = info[2 * blocks + step]
    at = info[blocks + own]
    key_index = lax.broadcasted_iota(jnp.int32, (2 * rows, rows), 0) % rows
    query_index = lax.broadcasted_iota(jnp.int32, (2 * rows, rows), 1)
    allowed = key_index <= query_index
    top_half = lax.broadcasted_iota(jnp.int32, (2 * rows, rows), 0) < rows

    products = att_ref[...].astype(F32) * grad_ref[...].astype(F32)
    head_row = lax.broadcasted_iota(jnp.int32, (2 * pairs, query_width), 0)
    head_col = lax.broadcasted_iota(jnp.int32, (2 * pairs, query_width), 1) // HD
    picker = jnp.where(head_row == head_col, 1.0, 0.0)
    delta_s[...] = lax.dot_general(
        picker, products, (((1,), (1,)), ((), ())),
        precision=lax.Precision.HIGHEST, preferred_element_type=F32,
    )

    def one_block(where_, masked):
        keys = keys_s[where_]
        values = values_s[where_]
        for pair in range(pairs):
            cols = pl.ds(pair * 128, 128)
            query = query_ref[:, cols]
            grad = grad_ref[:, cols]
            lse = jnp.where(
                top_half, lse_ref[2 * pair : 2 * pair + 1, :], lse_ref[2 * pair + 1 : 2 * pair + 2, :]
            )
            delta = jnp.where(
                top_half, delta_s[2 * pair : 2 * pair + 1, :], delta_s[2 * pair + 1 : 2 * pair + 2, :]
            )
            scores = mm_nt(keys, query) - lse
            if masked:
                scores = jnp.where(allowed, scores, NEG)
            probs = jnp.exp(scores)
            grad_probs = mm_nt(values, grad)
            grad_scores = (probs * (grad_probs - delta)).astype(BF16)
            value_acc[where_] += mm(probs.astype(BF16), grad)
            key_acc[where_] += mm(grad_scores, query)
            part = mm_tn(grad_scores, keys)
            if masked:
                query_acc[:, cols] = part
            else:
                query_acc[:, cols] += part

    one_block(at, True)
    for back in range(1, blocks):

        @pl.when(own - back >= low)
        def _():
            one_block(info[blocks + jnp.maximum(own - back, 0)], False)

    for pair in range(pairs):
        cols = pl.ds(pair * 128, 128)
        grad = query_acc[:, cols].astype(BF16).astype(F32)
        out_ref[:, cols] = (grad * cos_ref[...] - swap_halves(grad) * sin_ref[...]).astype(BF16)

    if final:

        @pl.when(step == first + pl.num_programs(0) - 1)
        def _():
            lane = lax.broadcasted_iota(jnp.int32, (rows, 128), 1)
            for part in range(blocks):
                spot = pl.ds(part * rows, rows)
                key_grad = key_acc[part]
                key_grad = key_grad[:rows] + pltpu.roll(key_grad[rows:], HD, 1)
                key_grad = (key_grad * (1.0 / math.sqrt(HD))).astype(BF16).astype(F32)
                value_grad = value_acc[part]
                value_grad = pltpu.roll(value_grad[:rows], HD, 1) + value_grad[rows:]
                turned = key_grad * cos_all[spot, :] - swap_halves(key_grad) * sin_all[spot, :]
                kv_out[spot, :] = jnp.where(lane < HD, turned, value_grad).astype(BF16)


def attention_backward(info, query, attended, grad, lse, kv, cosine, sine, rows, first, count, carried):
    total, query_width = query.shape
    blocks = total // rows
    pairs = query_width // 128
    final = first + count == blocks
    row_block = pl.BlockSpec((rows, query_width), lambda j, info: (j + first, 0))
    table_block = pl.BlockSpec((rows, 128), lambda j, info: (j + first, 0))
    whole = pl.BlockSpec((total, 128), lambda j, info: (0, 0))
    sums = pl.BlockSpec((blocks, 2 * rows, 128), lambda j, info: (0, 0, 0))
    sums_shape = jax.ShapeDtypeStruct((blocks, 2 * rows, 128), F32)
    in_specs = [
        row_block, row_block,
        pl.BlockSpec((rows, query_width), lambda j, info: (j, 0)),
        pl.BlockSpec((2 * pairs, rows), lambda j, info: (0, j + first)),
        whole, table_block, table_block, whole, whole,
    ]
    operands = [info, query, attended, grad, lse, kv, cosine, sine, cosine, sine]
    aliases = {}
    if first:
        aliases = {len(operands): 0, len(operands) + 1: 1, len(operands) + 2: 2}
        operands += carried
        in_specs += [pl.BlockSpec(memory_space=pl.ANY), sums, sums]
    out_specs = [row_block, sums, sums]
    out_shape = [jax.ShapeDtypeStruct((total, query_width + 128), BF16), sums_shape, sums_shape]
    if final:
        out_specs.append(whole)
        out_shape.append(jax.ShapeDtypeStruct((total, 128), BF16))
    return pl.pallas_call(
        functools.partial(attention_backward_kernel, first, final),
        grid_spec=pltpu.PrefetchScalarGridSpec(
            num_scalar_prefetch=1,
            grid=(count,),
            in_specs=in_specs,
            out_specs=out_specs,
            scratch_shapes=[
                pltpu.VMEM((blocks, 2 * rows, 128), BF16),
                pltpu.VMEM((blocks, 2 * rows, 128), BF16),
                pltpu.VMEM((rows, query_width), F32),
                pltpu.VMEM((2 * pairs, rows), F32),
            ],
        ),
        out_shape=out_shape,
        input_output_aliases=aliases,
        cost_estimate=pl.CostEstimate(flops=count * 6 * 10**9, bytes_accessed=count * 10**6, transcendentals=0),
        name="attention_backward",
    )(*operands)


def feed_forward_kernel(values_ref, grad_ref, gate_w, up_w, *refs):
    rows_out, mixed_ref, gate_ref, up_ref, back_ref = refs[-5:]
    width = values_ref.shape[1]
    hidden = gate_w.shape[1]
    rows_out[...] = values_ref[...]

    def columns(first, size):
        cols = pl.ds(first, size)
        values = values_ref[...]
        gate = mm(values, gate_w[:, cols])
        upward = mm(values, up_w[:, cols])
        grad = grad_ref[:, cols]
        sigma = 1.0 / (1.0 + jnp.exp(-gate))
        activated = gate * sigma
        mixed_ref[:, cols] = (activated * upward).astype(BF16)
        gate_ref[:, cols] = (grad * upward * sigma * (1.0 + gate * (1.0 - sigma))).astype(BF16)
        up_ref[:, cols] = (grad * activated).astype(BF16)

    step = min(256, hidden)

    @pl.loop(0, hidden // step)
    def _(index):
        columns(pl.multiple_of(index * step, step), step)

    if hidden % step:
        columns(hidden - hidden % step, hidden % step)

    part = min(256, width)

    @pl.loop(0, width // part)
    def _(index):
        here = pl.ds(pl.multiple_of(index * part, part), part)
        back_ref[:, here] = (
            mm_nt(gate_ref[...], gate_w[here, :]) + mm_nt(up_ref[...], up_w[here, :])
        ).astype(BF16)


def feed_forward(values, grad_mixed, gate_weight, up_weight, block, blocks, carried):
    rows, width = values.shape
    hidden = gate_weight.shape[1]
    here = pl.BlockSpec((rows, hidden), lambda i: (block, 0))
    resident = pl.BlockSpec(memory_space=pltpu.VMEM)
    operands = [values, grad_mixed, gate_weight, up_weight, *carried]
    whole = jax.ShapeDtypeStruct((blocks * rows, hidden), BF16)
    return pl.pallas_call(
        feed_forward_kernel,
        grid=(1,),
        in_specs=[
            pl.BlockSpec((rows, width), lambda i: (0, 0)), here, resident, resident,
            *[pl.BlockSpec(memory_space=pl.ANY)] * len(carried),
        ],
        out_specs=[
            pl.BlockSpec((rows, width), lambda i: (block, 0)), here, here, here,
            pl.BlockSpec((rows, width), lambda i: (0, 0)),
        ],
        out_shape=[
            jax.ShapeDtypeStruct((blocks * rows, width), BF16), whole, whole, whole,
            jax.ShapeDtypeStruct((rows, width), BF16),
        ],
        input_output_aliases={4 + i: i for i in range(len(carried))},
        cost_estimate=pl.CostEstimate(flops=6 * 10**9, bytes_accessed=10**6, transcendentals=0),
        name="feed_forward",
    )(*operands)


def norm_scale(values):
    return lax.rsqrt(jnp.mean(values * values, axis=-1, keepdims=True) + EPS)


def norm_backward(values, scale, gain, grads):
    weighted = grads * gain
    gain_grad = jnp.sum(grads * values * scale, axis=0)
    cubed = scale * scale * scale
    value_grad = scale * weighted - values * cubed * jnp.mean(weighted * values, axis=-1, keepdims=True)
    return gain_grad, value_grad


def over_batch(term):
    return lax.psum_scatter(term, "batch", scatter_dimension=0, tiled=True).astype(F32)


def pick(parts, index, axis):
    return lax.dynamic_index_in_dim(parts, index, axis, keepdims=False)


def line_sum(term):
    batch_parts = lax.axis_size("batch")
    line = batch_parts // 2
    index = lax.axis_index("batch")
    core, place = index % 2, index // 2
    parts = term.reshape(line, 2, term.shape[0] // batch_parts, term.shape[1])
    swap = [(i, i ^ 1) for i in range(batch_parts)]
    arrived = lax.ppermute(pick(parts, 1 - core, 1), "batch", swap)
    parts = (pick(parts, core, 1).astype(F32) + arrived.astype(F32)).astype(BF16)
    up = down = None
    for step in range(1, line):
        rising = pick(parts, jnp.minimum(place + line - step, line - 1), 0)
        falling = pick(parts, jnp.maximum(place - line + step, 0), 0)
        if up is not None:
            rising = (rising.astype(F32) + up.astype(F32)).astype(BF16)
            falling = (falling.astype(F32) + down.astype(F32)).astype(BF16)
        up = lax.ppermute(rising, "batch", [(i, i + 2) for i in range(2 * step)])
        down = lax.ppermute(
            falling, "batch", [(i, i - 2) for i in range(batch_parts - 2 * step, batch_parts)]
        )
    total = pick(parts, place, 0).astype(F32)
    if up is not None:
        total = total + up.astype(F32) + down.astype(F32)
    return total


def shards(
    tokens, seq_count, query_weight, key_weight, value_weight, out_weight,
    gate_weight, up_weight, down_weight, attention_gain, feedforward_gain, cotangent,
):
    seq_parts = lax.axis_size("seq")
    batch_parts = lax.axis_size("batch")
    part = lax.axis_index("seq")
    parity = lax.axis_index("batch") % 2
    rows = tokens.shape[1]
    group_rows = rows * seq_parts
    width = tokens.shape[2]

    order = jnp.arange(seq_parts, dtype=jnp.int32)
    swapped = ((order & 1) << 1) | (order >> 1)
    masks = jnp.where(parity == 0, order, swapped)
    owners = part ^ masks
    other = part ^ order
    spots = jnp.where(parity == 0, other, ((other & 1) << 1) | (other >> 1))
    seq_length = group_rows // seq_count[0]
    firsts = (owners * rows) // seq_length * seq_length // rows
    info = jnp.concatenate([owners, spots, firsts]).astype(jnp.int32)

    index = (owners[:, None] * rows + jnp.arange(rows, dtype=jnp.int32)[None, :]).reshape(-1)
    places = index - index // seq_length * seq_length
    lane = jnp.arange(128, dtype=jnp.int32)
    inverse = jnp.exp((lane % (HD // 2)).astype(F32) * (-2.0 * math.log(10000.0) / HD))
    angles = places.astype(F32)[:, None] * inverse[None, :]
    cosine = jnp.cos(angles)
    sine = jnp.sin(angles) * jnp.where(lane % HD < HD // 2, -1.0, 1.0)[None, :]

    inputs = tokens[0].astype(F32)
    scale_one = norm_scale(inputs)
    normed_one = (inputs * scale_one * attention_gain).astype(BF16)
    qkv_weight = jnp.concatenate([query_weight, key_weight, value_weight], axis=1)
    half = group_rows // 2

    near = first_swap(normed_one)
    side = second_swap(normed_one)
    qkv_own = mm(normed_one, qkv_weight)
    far = second_swap(after(near, qkv_own))
    normed_one_blocks = [normed_one, near, side, far]
    qkv = jnp.concatenate([qkv_own, *(mm(block, qkv_weight) for block in normed_one_blocks[1:])], axis=0)

    grad_ffn = after(cotangent[0], far)
    grad_near = first_swap(grad_ffn)
    grad_side = second_swap(grad_ffn)

    att_upper, query_upper, kv, lse_upper = attention_forward(info, qkv, cosine, sine, rows, seq_parts // 2, seq_parts // 2)
    branch_upper = mm(att_upper, out_weight).astype(BF16)
    arrived = second_swap(branch_upper)
    later_qkv, grad_near, grad_side = lax.optimization_barrier((after(qkv, branch_upper), grad_near, grad_side))
    grad_far = second_swap(grad_near)
    att_lower, query_lower, _, lse_lower = attention_forward(info, later_qkv, cosine, sine, rows, 0, seq_parts // 2)
    branch_lower = mm(att_lower, out_weight).astype(BF16)
    attended = jnp.concatenate([att_lower, att_upper], axis=0)
    query = jnp.concatenate([query_lower, query_upper], axis=0)
    lse = jnp.concatenate([lse_lower, lse_upper], axis=1)
    branch, passed = split_sum(branch_lower, after(arrived, branch_lower))
    passed = first_swap(after(passed, grad_far))
    grad_rows = jnp.concatenate([cotangent[0], grad_near, grad_side, grad_far], axis=0)
    grad_mixed = mm_nt(grad_rows, down_weight)
    hidden = inputs + branch + after(passed, grad_mixed).astype(F32)

    scale_two = norm_scale(hidden)
    normed_two = (hidden * scale_two * feedforward_gain).astype(BF16)
    near = first_swap(normed_two)
    side = second_swap(normed_two)
    *carried, back_own = feed_forward(normed_two, grad_mixed, gate_weight, up_weight, 0, seq_parts, [])
    near, side, *carried = lax.optimization_barrier((near, side, *carried))
    far = second_swap(near)
    *carried, back_near = feed_forward(near, grad_mixed, gate_weight, up_weight, 1, seq_parts, carried)
    *carried, back_side = feed_forward(side, grad_mixed, gate_weight, up_weight, 2, seq_parts, carried)
    sum_side = second_swap(back_side)
    *carried, back_far = feed_forward(far, grad_mixed, gate_weight, up_weight, 3, seq_parts, carried)
    normed_two_rows, mixed, grad_gate, grad_upward = carried
    sum_far = second_swap(back_far)
    down_term = mm_tn(mixed, after(grad_rows, back_far)).astype(BF16)
    passed = (back_near.astype(F32) + after(sum_far, down_term).astype(F32)).astype(BF16)
    passed = first_swap(passed)
    gate_term = mm_tn(normed_two_rows, after(grad_gate, down_term)).astype(BF16)
    grad_normed_two = back_own.astype(F32) + sum_side.astype(F32) + after(passed, gate_term).astype(F32)
    down_grad = over_batch(down_term)
    gate_grad = over_batch(gate_term)

    grad_out = cotangent[0].astype(F32)
    feed_gain_term, grad_hidden_norm = norm_backward(hidden, scale_two, feedforward_gain, grad_normed_two)
    grad_hidden = grad_out + grad_hidden_norm
    grad_branch = grad_hidden.astype(BF16)
    near = first_swap(grad_branch)
    side = second_swap(grad_branch)
    up_term = mm_tn(normed_two_rows, after(grad_upward, gate_term)).astype(BF16)
    up_grad = over_batch(up_term)

    def attended_grad(block):
        return mm_nt(block, out_weight).astype(BF16)

    def backward(grad, first, count, carried):
        return attention_backward(
            info, query, attended, grad, lse, kv, cosine, sine, rows, first, count, carried
        )

    ffn_upper = mm(after(mixed, up_term)[half:], down_weight).astype(BF16)
    carried = backward(after(attended_grad(grad_branch), ffn_upper), 0, 1, [])
    near, side, *carried = lax.optimization_barrier((near, side, *carried))
    far = second_swap(near)
    middle = attended_grad(jnp.concatenate([near, side], axis=0))
    carried = backward(middle, 1, 2, carried)
    far = after(far, *carried)
    ffn_arrived = second_swap(after(ffn_upper, far))
    grad_qkv, _, _, grad_kv = backward(attended_grad(far), 3, 1, carried)
    grad_qkv = lax.dynamic_update_slice(grad_qkv, grad_kv, (0, grad_qkv.shape[1] - grad_kv.shape[1]))
    upper = mm_nt(grad_qkv[half:], qkv_weight).astype(BF16)
    arrived = second_swap(after(upper, ffn_arrived))
    lower = mm_nt(grad_qkv[:half], qkv_weight).astype(BF16)
    grad_branch_rows = jnp.concatenate([grad_branch, near, side, far], axis=0)
    out_term = mm_tn(attended, after(grad_branch_rows, upper)).astype(BF16)
    normed_one_rows = jnp.concatenate(normed_one_blocks, axis=0)
    qkv_term = mm_tn(normed_one_rows, after(grad_qkv, upper)).astype(BF16)
    out_grad = line_sum(out_term)
    qkv_grad = line_sum(qkv_term)
    kept, passed = split_sum(lower, after(arrived, qkv_term, lower))
    passed = first_swap(passed)
    ffn_lower = mm(after(mixed, upper)[:half], down_weight).astype(BF16)
    ffn_kept, ffn_passed = split_sum(ffn_lower, ffn_arrived)
    ffn_passed = first_swap(ffn_passed)
    grad_normed_one = kept + passed.astype(F32)
    attention_gain_term, grad_inputs_norm = norm_backward(inputs, scale_one, attention_gain, grad_normed_one)
    input_grad = grad_hidden + grad_inputs_norm
    layer_out = (hidden + ffn_kept + ffn_passed.astype(F32)).astype(BF16)

    devices = seq_parts * batch_parts
    gains = jnp.concatenate(
        [attention_gain_term.reshape(devices, -1), feed_gain_term.reshape(devices, -1)], axis=1
    )
    gains = jnp.sum(lax.all_to_all(gains, ("seq", "batch"), 0, 0, tiled=True), axis=0)
    share = width // devices
    query_width = query_weight.shape[1]
    key_width = key_weight.shape[1]
    return (
        layer_out[None],
        input_grad[None],
        qkv_grad[:, :query_width],
        qkv_grad[:, query_width : query_width + key_width],
        qkv_grad[:, query_width + key_width :],
        out_grad,
        gate_grad,
        up_grad,
        down_grad,
        gains[:share],
        gains[share:],
    )


def solution(mesh):
    return jax.shard_map(
        shards,
        mesh=mesh,
        in_specs=(
            P("batch", "seq", None),
            P("batch"),
            P(None, "seq"),
            P(None, "seq"),
            P(None, "seq"),
            P("seq", None),
            P(None, "seq"),
            P(None, "seq"),
            P("seq", None),
            P(),
            P(),
            P("batch", "seq", None),
        ),
        out_specs=(
            P("batch", "seq", None),
            P("batch", "seq", None),
            P("batch", "seq"),
            P("batch", "seq"),
            P("batch", "seq"),
            P(("seq", "batch"), None),
            P("batch", "seq"),
            P("batch", "seq"),
            P(("seq", "batch"), None),
            P(("seq", "batch")),
            P(("seq", "batch")),
        ),
        check_vma=False,
    )
```

time: 680 us -> 514 us (0.76)
  waiting for transfers between devices: 374 us -> 146 us
  Pallas kernels: 54.4 us -> 117 us
  matrix products: 142 us -> 92.1 us
  starting transfers between devices: 32.6 us -> 52.6 us
  other arithmetic: 37.8 us -> 56.9 us
  local copies, waits for them, and re-layouts: 12.6 us -> 26 us
    ppermute x20 -> x21, waiting for transfers between devices: 247 us -> 96.3 us  [exchange(): return lax.ppermute(values, ('seq', 'batch'), pairs)]
    reduce_scatter x5 -> x3, waiting for transfers between devices: 124 us -> 0.01 us  [over_batch(): lax.psum_scatter(term, 'batch', scatter_dimension=0, tiled=True).astype(F32)]
    pallas_call x2 -> x9, Pallas kernels: 54.4 us -> 117 us  [the longest x4 63.7 us: feed_forward(): pl.pallas_call(feed_forward_kernel, grid=(1,), in_specs=[pl.BlockSpec((ro...]
    ppermute x0 -> x14, waiting for transfers between devices: none -> 46.3 us  [the longest x6 38.9 us: line_sum(): up = lax.ppermute(rising, 'batch', [(i, i + 2) for i in range(2 * step)])]
    ppermute x0 -> x14, starting transfers between devices: none -> 29.6 us  [the longest x6 23.5 us: line_sum(): up = lax.ppermute(rising, 'batch', [(i, i + 2) for i in range(2 * step)])]
    dot_general x8 -> x6, matrix products: 51.3 us -> 24.5 us  [mm_nt(): lax.dot_general(a, b, (((1,), (1,)), ((), ())), preferred_element_type=F32)]
    dot_general x10 -> x8, matrix products: 47 us -> 27 us  [mm(): lax.dot_general(a, b, (((1,), (0,)), ((), ())), preferred_element_type=F32)]
    ppermute x20 -> x21, starting transfers between devices: 29.6 us -> 19.9 us  [exchange(): return lax.ppermute(values, ('seq', 'batch'), pairs)]
  transfers between devices with their start and end apart: 26 -> 39, of which waited for: 17 -> 18; matrix products, arithmetic and copies ran while one was open for 20% -> 25% of each run, Pallas kernels for 4% -> 20%
where the time goes in v2:
time: 514 us; the launch traced here: 506 us
  waiting for transfers between devices  146 us (28%)
  Pallas kernels  117 us (23%)
  matrix products  92.1 us (18%)
  other arithmetic  56.9 us (11%)
  starting transfers between devices  52.6 us (10%)
  local copies, waits for them, and re-layouts  26 us (5%)
  between operations  15.5 us (3%)
    ppermute x21, waiting for transfers between devices, exchange(): return lax.ppermute(values, ('seq', 'batch'), pairs)  96.3 us
    pallas_call x4, Pallas kernels, feed_forward(): pl.pallas_call(feed_forward_kernel, grid=(1,), in_specs=[pl.BlockSpec((ro...  63.7 us
    dot_general x5, matrix products, mm_tn(): lax.dot_general(a, b, (((0,), (0,)), ((), ())), preferred_element_type=F32)  40.6 us
    ppermute x6, waiting for transfers between devices, line_sum(): up = lax.ppermute(rising, 'batch', [(i, i + 2) for i in range(2 * step)])  38.9 us
    pallas_call x3, Pallas kernels, attention_backward(): pl.pallas_call(functools.partial(attention_backward_kernel, first, final)...  34.7 us
    dot_general x8, matrix products, mm(): lax.dot_general(a, b, (((1,), (0,)), ((), ())), preferred_element_type=F32)  27 us
    dot_general x6, matrix products, mm_nt(): lax.dot_general(a, b, (((1,), (1,)), ((), ())), preferred_element_type=F32)  24.5 us
    ppermute x6, starting transfers between devices, line_sum(): up = lax.ppermute(rising, 'batch', [(i, i + 2) for i in range(2 * step)])  23.5 us
  transfers between devices with their start and end apart: 39, of which 18 were waited for; matrix products, arithmetic and copies ran while one was open for 25% of the time, Pallas kernels for 20%

profile of v2, /device:TPU:0, one launch (start us, length us, event | category | flops | bytes accessed | tf_op | source)
XLA Modules:
  0.0 506.4 jit_solution(6265612182963187829)
XLA Ops:
  12.0 3.0 collective-permute-start
  19.8 3.0 fusion.67
  23.1 15.6 %collective-permute-done = bf16[256,2048]{1,0:T(8,128)(2,1)} collective-permute-done((bf16[256,2048]{1,0:T(8,128)(2,1)}, bf16[256,2048]{1,0:T(8,128)(2,1)}, u32[]{:S(2)}, u32[]{:S(2)}) %collective-permute-start) | collective-permute-done | bytes 1048608 | tf_op jit(solution)/shard_map/ppermute | solution.py:38
  40.8 3.1 fusion.43
  48.4 5.3 %collective-permute-done.2 = bf16[256,2048]{1,0:T(8,128)(2,1)S(1)} collective-permute-done((bf16[256,2048]{1,0:T(8,128)(2,1)}, bf16[256,2048]{1,0:T(8,128)(2,1)S(1)}, u32[]{:S(2)}, u32[]{:S(2)}) %collective-permute-start.2) | collective-permute-done | bytes 1048608 | tf_op jit(solution)/shard_map/ppermute | solution.py:38
  53.8 2.8 collective-permute-start.3
  59.8 11.4 %attention_forward.2 = (bf16[512,512]{1,0:T(8,128)(2,1)}, bf16[512,512]{1,0:T(8,128)(2,1)}, bf16[1024,128]{1,0:T(8,128)(2,1)}, f32[8,512]{1,0:T(8,128)}) custom-call(s32[12]{0:T(128)} %pad_add_fusion.info, f32[1024,640]{1,0:T(8,128)} %pad_maximum_fusion.3.query_ref.kv_ref, f32[1024,640]{1,0:T(8,128)} %pad_maximum_fusion.3.query_ref.kv_ref, ...), custom_call_target="tpu_custom_call" | custom-call | flops 8000000000 | bytes 2000000 | tf_op jit(solution)/shard_map/attention_forward/pallas_call | solution.py:168
  71.2 3.6 convolution_convert_fusion.5
  74.8 5.9 %collective-permute-done.3 = bf16[256,2048]{1,0:T(8,128)(2,1)} collective-permute-done((bf16[256,2048]{1,0:T(8,128)(2,1)S(1)}, bf16[256,2048]{1,0:T(8,128)(2,1)}, u32[]{:S(2)}, u32[]{:S(2)}) %collective-permute-start.3) | collective-permute-done | bytes 1048608 | tf_op jit(solution)/shard_map/ppermute | solution.py:38
  81.5 7.6 %attention_forward.3 = (bf16[512,512]{1,0:T(8,128)(2,1)}, bf16[512,512]{1,0:T(8,128)(2,1)}, bf16[1024,128]{1,0:T(8,128)(2,1)}, f32[8,512]{1,0:T(8,128)}) custom-call(s32[12]{0:T(128)} %pad_add_fusion.info, f32[1024,640]{1,0:T(8,128)} %pad_maximum_fusion.3.query_ref.kv_ref, f32[1024,640]{1,0:T(8,128)} %pad_maximum_fusion.3.query_ref.kv_ref, ...), custom_call_target="tpu_custom_call" | custom-call | flops 8000000000 | bytes 2000000 | tf_op jit(solution)/shard_map/attention_forward/pallas_call | solution.py:168
  91.5 9.6 %collective-permute-done.5 = bf16[512,2048]{1,0:T(8,128)(2,1)} collective-permute-done((bf16[512,2048]{1,0:T(8,128)(2,1)}, bf16[512,2048]{1,0:T(8,128)(2,1)}, u32[]{:S(2)}, u32[]{:S(2)}) %collective-permute-start.5) | collective-permute-done | bytes 2097184 | tf_op jit(solution)/shard_map/ppermute | solution.py:38
  103.7 8.7 %collective-permute-done.6 = bf16[256,2048]{1,0:T(8,128)(2,1)} collective-permute-done((bf16[256,2048]{1,0:T(8,128)(2,1)}, bf16[256,2048]{1,0:T(8,128)(2,1)}, u32[]{:S(2)}, u32[]{:S(2)}) %collective-permute-start.6) | collective-permute-done | bytes 1048608 | tf_op jit(solution)/shard_map/ppermute | solution.py:38
  113.1 10.8 %fusion.61.grad_ref = f32[1024,1408]{1,0:T(8,128)} fusion(bf16[1408,2048]{1,0:T(8,128)(2,1)S(1)} %bitcast.114, bf16[256,2048]{1,0:T(8,128)(2,1)} %collective-permute-done.6, bf16[256,2048]{1,0:T(8,128)(2,1)} %collective-permute-done.4, bf16[256,2048]{1,0:T(8,128)(2,1)} %collective-permute-done.3, bf16[256,2048]{1,0:T(8,128)(2,1)S(1)} %bitcast.106), kind=kOutput, calls=%fused_computation.147 | convolution fusion | flops 5922357248 | bytes 15728640 | tf_op jit(solution)/shard_map/dot_general | solution.py:23
  123.9 3.3 collective-permute-done.7
  131.2 3.6 pad_maximum_fusion
  134.8 15.9 %feed_forward.4 = (bf16[1024,2048]{1,0:T(8,128)(2,1)}, bf16[1024,1408]{1,0:T(8,128)(2,1)}, bf16[1024,1408]{1,0:T(8,128)(2,1)}, bf16[1024,1408]{1,0:T(8,128)(2,1)}, bf16[256,2048]{1,0:T(8,128)(2,1)}) custom-call(bf16[256,2048]{1,0:T(8,128)(2,1)} %multiply_convert_fusion.values_ref, f32[1024,1408]{1,0:T(8,128)} %fusion.61.grad_ref, bf16[2048,1408]{1,0:T(8,128)(2,1)} %gate_w.7, ...), custom_call_target="tpu_custom_call" | custom-call | flops 6000000000 | bytes 1000000 | tf_op jit(solution)/shard_map/feed_forward/pallas_call | solution.py:403
  150.7 3.7 collective-permute-done.8.values_ref
  155.6 15.9 %feed_forward.5 = (bf16[1024,2048]{1,0:T(8,128)(2,1)}, bf16[1024,1408]{1,0:T(8,128)(2,1)}, bf16[1024,1408]{1,0:T(8,128)(2,1)}, bf16[1024,1408]{1,0:T(8,128)(2,1)}, bf16[256,2048]{1,0:T(8,128)(2,1)}) custom-call(bf16[256,2048]{1,0:T(8,128)(2,1)} %collective-permute-done.8.values_ref, ...), custom_call_target="tpu_custom_call", output_to_operand_aliasing={{0}: (4, {}), {1}: (5, {}), {2}: (6, {}), {3}: (7, {})} | custom-call | flops 6000000000 | bytes 1000000 | tf_op jit(solution)/shard_map/feed_forward/pallas_call | solution.py:403
  171.5 15.9 %feed_forward.6 = (bf16[1024,2048]{1,0:T(8,128)(2,1)}, bf16[1024,1408]{1,0:T(8,128)(2,1)}, bf16[1024,1408]{1,0:T(8,128)(2,1)}, bf16[1024,1408]{1,0:T(8,128)(2,1)}, bf16[256,2048]{1,0:T(8,128)(2,1)}) custom-call(bf16[256,2048]{1,0:T(8,128)(2,1)} %collective-permute-done.9.values_ref, ...), custom_call_target="tpu_custom_call", output_to_operand_aliasing={{0}: (4, {}), {1}: (5, {}), {2}: (6, {}), {3}: (7, {})} | custom-call | flops 6000000000 | bytes 1000000 | tf_op jit(solution)/shard_map/feed_forward/pallas_call | solution.py:403
  188.4 15.9 %feed_forward.7 = (bf16[1024,2048]{1,0:T(8,128)(2,1)}, bf16[1024,1408]{1,0:T(8,128)(2,1)}, bf16[1024,1408]{1,0:T(8,128)(2,1)}, bf16[1024,1408]{1,0:T(8,128)(2,1)}, bf16[256,2048]{1,0:T(8,128)(2,1)}) custom-call(bf16[256,2048]{1,0:T(8,128)(2,1)} %copy-done.18, ...), custom_call_target="tpu_custom_call", output_to_operand_aliasing={{0}: (4, {}), {1}: (5, {}), {2}: (6, {}), {3}: (7, {})} | custom-call | flops 6000000000 | bytes 1000000 | tf_op jit(solution)/shard_map/feed_forward/pallas_call | solution.py:403
  204.3 10.4 %convolution_convert_fusion.2 = bf16[1408,2048]{1,0:T(8,128)(2,1)} fusion(bf16[1024,1408]{1,0:T(8,128)(2,1)} %get-tuple-element.143, bf16[1024,2048]{1,0:T(8,128)(2,1)} %pad_maximum_fusion), kind=kOutput, calls=%fused_computation.2 | convolution fusion | flops 5908463616 | bytes 12845056 | tf_op jit(solution)/shard_map/dot_general | solution.py:27
  214.7 11.0 %convolution_convert_fusion.1 = bf16[2048,1408]{1,0:T(8,128)(2,1)} fusion(bf16[1024,2048]{1,0:T(8,128)(2,1)} %get-tuple-element.118, bf16[1024,1408]{1,0:T(8,128)(2,1)} %get-tuple-element.120), kind=kOutput, calls=%fused_computation.1 | convolution fusion | flops 5908463616 | bytes 12845056 | tf_op jit(solution)/shard_map/dot_general | solution.py:27
  225.7 11.2 %convolution_convert_fusion = bf16[2048,1408]{1,0:T(8,128)(2,1)} fusion(bf16[1024,2048]{1,0:T(8,128)(2,1)} %get-tuple-element.118, bf16[1024,1408]{1,0:T(8,128)(2,1)} %get-tuple-element.123), kind=kOutput, calls=%fused_computation | convolution fusion | flops 5908463616 | bytes 12845056 | tf_op jit(solution)/shard_map/dot_general | solution.py:27
  238.7 14.1 %collective-permute-done.12 = bf16[256,2048]{1,0:T(8,128)(2,1)S(1)} collective-permute-done((bf16[256,2048]{1,0:T(8,128)(2,1)}, bf16[256,2048]{1,0:T(8,128)(2,1)S(1)}, u32[]{:S(2)}, u32[]{:S(2)}) %collective-permute-start.12) | collective-permute-done | bytes 1048608 | tf_op jit(solution)/shard_map/ppermute | solution.py:38
  261.4 18.3 %collective-permute-done.13 = bf16[256,2048]{1,0:T(8,128)(2,1)} collective-permute-done((bf16[256,2048]{1,0:T(8,128)(2,1)}, bf16[256,2048]{1,0:T(8,128)(2,1)}, u32[]{:S(2)}, u32[]{:S(2)}) %collective-permute-start.13) | collective-permute-done | bytes 1048608 | tf_op jit(solution)/shard_map/ppermute | solution.py:38
  282.4 4.3 fusion.62
  287.4 7.4 %convolution_convert_fusion.9 = bf16[512,2048]{1,0:T(8,128)(2,1)} fusion(bf16[1408,2048]{1,0:T(8,128)(2,1)} %param.20, bf16[1024,1408]{1,0:T(8,128)(2,1)S(1)} %copy-done.5), kind=kOutput, calls=%fused_computation.29 | convolution fusion | flops 2953838592 | bytes 9306112 | tf_op jit(solution)/shard_map/dot_general | solution.py:19
  297.5 7.0 %attention_backward.3 = (bf16[1024,640]{1,0:T(8,128)(2,1)}, f32[4,512,128]{2,1,0:T(8,128)}, f32[4,512,128]{2,1,0:T(8,128)}) custom-call(s32[12]{0:T(128)} %pad_add_fusion.info, bf16[1024,512]{1,0:T(8,128)(2,1)} %copy-done.23, bf16[1024,512]{1,0:T(8,128)(2,1)} %copy-done.21, bf16[256,512]{1,0:T(8,128)(2,1)} %convolution_convert_fusion.11.grad_ref, ...), custom_call_target="tpu_custom_call" | custom-call | flops 6000000000 | bytes 1000000 | tf_op jit(solution)/shard_map/attention_backward/pallas_call | solution.py:338
  304.5 6.9 %collective-permute-done.14 = bf16[256,2048]{1,0:T(8,128)(2,1)S(1)} collective-permute-done((bf16[256,2048]{1,0:T(8,128)(2,1)}, bf16[256,2048]{1,0:T(8,128)(2,1)S(1)}, u32[]{:S(2)}, u32[]{:S(2)}) %collective-permute-start.14) | collective-permute-done | bytes 1048608 | tf_op jit(solution)/shard_map/ppermute | solution.py:38
  313.2 3.3 fusion.32.grad_ref
  316.5 15.3 %attention_backward.4 = (bf16[1024,640]{1,0:T(8,128)(2,1)}, f32[4,512,128]{2,1,0:T(8,128)}, f32[4,512,128]{2,1,0:T(8,128)}) custom-call(s32[12]{0:T(128)} %pad_add_fusion.info, bf16[1024,512]{1,0:T(8,128)(2,1)} %copy-done.23, bf16[1024,512]{1,0:T(8,128)(2,1)} %copy-done.21, ...), custom_call_target="tpu_custom_call", output_to_operand_aliasing={{0}: (10, {}), {1}: (11, {}), {2}: (12, {})} | custom-call | flops 12000000000 | bytes 2000000 | tf_op jit(solution)/shard_map/attention_backward/pallas_call | solution.py:338
  334.5 12.4 %attention_backward.5 = (bf16[1024,640]{1,0:T(8,128)(2,1)}, f32[4,512,128]{2,1,0:T(8,128)}, f32[4,512,128]{2,1,0:T(8,128)}, bf16[1024,128]{1,0:T(8,128)(2,1)}) custom-call(s32[12]{0:T(128)} %pad_add_fusion.info, bf16[1024,512]{1,0:T(8,128)(2,1)} %copy-done.23, ...), custom_call_target="tpu_custom_call", output_to_operand_aliasing={{0}: (10, {}), {1}: (11, {}), {2}: (12, {})} | custom-call | flops 6000000000 | bytes 1000000 | tf_op jit(solution)/shard_map/attention_backward/pallas_call | solution.py:338
  351.7 3.1 convolution_convert_fusion.8
  359.6 5.7 %fusion.8 = bf16[2048,640]{1,0:T(8,128)(2,1)S(1)} fusion(bf16[1024,640]{1,0:T(8,128)(2,1)S(1)} %copy-done.34, bf16[256,2048]{1,0:T(8,128)(2,1)} %copy-done.36, bf16[256,2048]{1,0:T(8,128)(2,1)} %collective-permute-done.1, bf16[256,2048]{1,0:T(8,128)(2,1)} %collective-permute-done, bf16[256,2048]{1,0:T(8,128)(2,1)} %fusion.14), kind=kOutput, calls=%fused_computation.22 | convolution fusion | flops 2702442496 | bytes 8126464 | tf_op jit(solution)/shard_map/dot_general | solution.py:27
  376.8 7.4 %collective-permute-done.29 = bf16[64,2048]{1,0:T(8,128)(2,1)} collective-permute-done((bf16[64,2048]{1,0:T(8,128)(2,1)}, bf16[64,2048]{1,0:T(8,128)(2,1)}, u32[]{:S(2)}, u32[]{:S(2)}) %collective-permute-start.29) | collective-permute-done | bytes 262176 | tf_op jit(solution)/shard_map/ppermute | solution.py:460
  385.3 4.7 collective-permute-start.30
  394.0 8.2 %collective-permute-done.30 = bf16[64,2048]{1,0:T(8,128)(2,1)S(1)} collective-permute-done((bf16[64,2048]{1,0:T(8,128)(2,1)S(1)}, bf16[64,2048]{1,0:T(8,128)(2,1)S(1)}, u32[]{:S(2)}, u32[]{:S(2)}) %collective-permute-start.30) | collective-permute-done | bytes 262176 | tf_op jit(solution)/shard_map/ppermute | solution.py:460
  405.9 5.3 %collective-permute-start.31 = (bf16[64,2048]{1,0:T(8,128)(2,1)S(1)}, bf16[64,2048]{1,0:T(8,128)(2,1)S(1)}, u32[]{:S(2)}, u32[]{:S(2)}) collective-permute-start(bf16[64,2048]{1,0:T(8,128)(2,1)S(1)} %get-tuple-element.187), channel_id=1, source_target_pairs={{0,2},{1,3},{2,4},{3,5},{4,6},{5,7},{8,10},{9,11},{10,12},{11,13},... | collective-permute-start | bytes 786440 | tf_op jit(solution)/shard_map/ppermute | solution.py:460
  411.2 5.1 %collective-permute-done.22 = bf16[256,640]{0,1:T(8,128)(2,1)S(1)} collective-permute-done((bf16[256,640]{0,1:T(8,128)(2,1)S(1)}, bf16[256,640]{0,1:T(8,128)(2,1)S(1)}, u32[]{:S(2)}, u32[]{:S(2)}) %collective-permute-start.22) | collective-permute-done | bytes 327712 | tf_op jit(solution)/shard_map/ppermute | solution.py:460
  416.3 4.6 collective-permute-start.23
  422.5 18.1 %collective-permute-done.23 = bf16[256,640]{0,1:T(8,128)(2,1)S(1)} collective-permute-done((bf16[256,640]{0,1:T(8,128)(2,1)S(1)}, bf16[256,640]{0,1:T(8,128)(2,1)S(1)}, u32[]{:S(2)}, u32[]{:S(2)}) %collective-permute-start.23) | collective-permute-done | bytes 327712 | tf_op jit(solution)/shard_map/ppermute | solution.py:460
  441.5 5.0 collective-permute-start.24
  446.5 5.0 convert_add_fusion.2
  461.1 7.4 %collective-permute-done.27 = bf16[256,640]{0,1:T(8,128)(2,1)S(1)} collective-permute-done((bf16[256,640]{0,1:T(8,128)(2,1)S(1)}, bf16[256,640]{0,1:T(8,128)(2,1)S(1)}, u32[]{:S(2)}, u32[]{:S(2)}) %collective-permute-start.27) | collective-permute-done | bytes 327712 | tf_op jit(solution)/shard_map/ppermute | solution.py:461
  470.4 4.2 fusion.35
  474.5 4.7 collective-permute-done.20
  481.9 3.0 all-to-all-start
  485.0 4.5 fusion.19
  (212 shorter events, 108.4 us)
Async XLA Ops:
  7.2 64.0 %copy-start = (bf16[512,2048]{1,0:T(8,128)(2,1)S(1)}, bf16[512,2048]{1,0:T(8,128)(2,1)}, u32[]{:S(2)}) copy-start(bf16[512,2048]{1,0:T(8,128)(2,1)} %param.17) | copy-start | bytes 6291460
  7.2 485.5 %reduce-scatter.6.cloned.1.call-start = ((), (), s32[]{:S(2)}) async-start(), calls=%async_computation.5 | async-start | bytes 6488064 | tf_op jit(solution)/shard_map/reduce_scatter | solution.py:437
  12.0 26.7 %collective-permute-start = (bf16[256,2048]{1,0:T(8,128)(2,1)}, bf16[256,2048]{1,0:T(8,128)(2,1)}, u32[]{:S(2)}, u32[]{:S(2)}) collective-permute-start(bf16[256,2048]{1,0:T(8,128)(2,1)} %fusion.14), channel_id=1, source_target_pairs={{0,8},{1,17},{2,10},{3,19},{4,12},{5,21},{6,14},{7,23},{8,0},{9,25... | collective-permute-start | bytes 3145736 | tf_op jit(solution)/shard_map/ppermute | solution.py:38
  15.0 31.1 %collective-permute-start.1 = (bf16[256,2048]{1,0:T(8,128)(2,1)}, bf16[256,2048]{1,0:T(8,128)(2,1)}, u32[]{:S(2)}, u32[]{:S(2)}) collective-permute-start(bf16[256,2048]{1,0:T(8,128)(2,1)} %fusion.14), channel_id=1, source_target_pairs={{0,16},{1,9},{2,18},{3,11},{4,20},{5,13},{6,22},{7,15},{8,24},{9,1... | collective-permute-start | bytes 3145736 | tf_op jit(solution)/shard_map/ppermute | solution.py:38
  19.8 37.2 %copy-start.12 = (bf16[2048,640]{1,0:T(8,128)(2,1)}, bf16[2048,640]{1,0:T(8,128)(2,1)S(1)}, u32[]{:S(2)}) copy-start(bf16[2048,640]{1,0:T(8,128)(2,1)S(1)} %pad_maximum_fusion.2) | copy-start | bytes 7864324
  38.7 15.0 %collective-permute-start.2 = (bf16[256,2048]{1,0:T(8,128)(2,1)}, bf16[256,2048]{1,0:T(8,128)(2,1)S(1)}, u32[]{:S(2)}, u32[]{:S(2)}) collective-permute-start(bf16[256,2048]{1,0:T(8,128)(2,1)} %collective-permute-done), channel_id=1, source_target_pairs={{0,16},{1,9},{2,18},{3,11},{4,20},{5,13},{6,22},{7,15},{8,24},{9,1... | collective-permute-start | bytes 3145736 | tf_op jit(solution)/shard_map/ppermute | solution.py:38
  53.8 27.0 %collective-permute-start.3 = (bf16[256,2048]{1,0:T(8,128)(2,1)S(1)}, bf16[256,2048]{1,0:T(8,128)(2,1)}, u32[]{:S(2)}, u32[]{:S(2)}) collective-permute-start(bf16[256,2048]{1,0:T(8,128)(2,1)S(1)} %bitcast.104), channel_id=1, source_target_pairs={{0,8},{1,17},{2,10},{3,19},{4,12},{5,21},{6,14},{7,23},{8,0},{9,25... | collective-permute-start | bytes 3145736 | tf_op jit(solution)/shard_map/ppermute | solution.py:38
  56.6 24.1 %collective-permute-start.4 = (bf16[256,2048]{1,0:T(8,128)(2,1)S(1)}, bf16[256,2048]{1,0:T(8,128)(2,1)}, u32[]{:S(2)}, u32[]{:S(2)}) collective-permute-start(bf16[256,2048]{1,0:T(8,128)(2,1)S(1)} %bitcast.105), channel_id=1, source_target_pairs={{0,16},{1,9},{2,18},{3,11},{4,20},{5,13},{6,22},{7,15},{8,24},{9,1... | collective-permute-start | bytes 3145736 | tf_op jit(solution)/shard_map/ppermute | solution.py:38
  74.8 26.4 %collective-permute-start.5 = (bf16[512,2048]{1,0:T(8,128)(2,1)}, bf16[512,2048]{1,0:T(8,128)(2,1)}, u32[]{:S(2)}, u32[]{:S(2)}) collective-permute-start(bf16[512,2048]{1,0:T(8,128)(2,1)} %convolution_convert_fusion.5), channel_id=1, source_target_pairs={{0,16},{1,9},{2,18},{3,11},{4,20},{5,13},{6,22},{7,15},{8,24},{9,1... | collective-permute-start | bytes 6291464 | tf_op jit(solution)/shard_map/ppermute | solution.py:38
  80.7 31.7 %collective-permute-start.6 = (bf16[256,2048]{1,0:T(8,128)(2,1)}, bf16[256,2048]{1,0:T(8,128)(2,1)}, u32[]{:S(2)}, u32[]{:S(2)}) collective-permute-start(bf16[256,2048]{1,0:T(8,128)(2,1)} %collective-permute-done.3), channel_id=1, source_target_pairs={{0,16},{1,9},{2,18},{3,11},{4,20},{5,13},{6,22},{7,15},{8,24},{9,1... | collective-permute-start | bytes 3145736 | tf_op jit(solution)/shard_map/ppermute | solution.py:38
  89.1 24.0 %slice-start = ((s8[5767168]{0:T(1024)(128)(4,1)}), s8[4194304]{0:T(1024)(128)(4,1)S(1)}, s32[]{:S(2)}) async-start(s8[5767168]{0:T(1024)(128)(4,1)} %bitcast.113), calls=%async_computation.7 | async-start | bytes 8388608
  103.7 23.5 %copy-start.3 = (bf16[1,256,2048]{2,1,0:T(8,128)(2,1)S(1)}, bf16[1,256,2048]{2,1,0:T(8,128)(2,1)}, u32[]{:S(2)}) copy-start(bf16[1,256,2048]{2,1,0:T(8,128)(2,1)} %param.12) | copy-start | bytes 3145732
  112.4 14.8 %collective-permute-start.7 = (bf16[256,2048]{1,0:T(8,128)(2,1)S(1)}, bf16[256,2048]{1,0:T(8,128)(2,1)S(1)}, u32[]{:S(2)}, u32[]{:S(2)}) collective-permute-start(bf16[256,2048]{1,0:T(8,128)(2,1)S(1)} %slice.102), channel_id=1, source_target_pairs={{0,8},{1,17},{2,10},{3,19},{4,12},{5,21},{6,14},{7,23},{8,0},{9,25... | collective-permute-start | bytes 3145736 | tf_op jit(solution)/shard_map/ppermute | solution.py:38
  130.4 24.1 %collective-permute-start.8 = (bf16[256,2048]{1,0:T(8,128)(2,1)}, bf16[256,2048]{1,0:T(8,128)(2,1)}, u32[]{:S(2)}, u32[]{:S(2)}) collective-permute-start(bf16[256,2048]{1,0:T(8,128)(2,1)} %multiply_convert_fusion.values_ref), channel_id=1, source_target_pairs={{0,8},{1,17},{2,10},{3,19},{4,12},{5,21},{6,14},{7,23},{8,0},{9,25... | collective-permute-start | bytes 3145736 | tf_op jit(solution)/shard_map/ppermute | solution.py:38
  131.0 23.5 %collective-permute-start.9 = (bf16[256,2048]{1,0:T(8,128)(2,1)}, bf16[256,2048]{1,0:T(8,128)(2,1)}, u32[]{:S(2)}, u32[]{:S(2)}) collective-permute-start(bf16[256,2048]{1,0:T(8,128)(2,1)} %multiply_convert_fusion.values_ref), channel_id=1, source_target_pairs={{0,16},{1,9},{2,18},{3,11},{4,20},{5,13},{6,22},{7,15},{8,24},{9,1... | collective-permute-start | bytes 3145736 | tf_op jit(solution)/shard_map/ppermute | solution.py:38
  154.5 32.9 %collective-permute-start.10 = (bf16[256,2048]{1,0:T(8,128)(2,1)}, bf16[256,2048]{1,0:T(8,128)(2,1)S(1)}, u32[]{:S(2)}, u32[]{:S(2)}) collective-permute-start(bf16[256,2048]{1,0:T(8,128)(2,1)} %collective-permute-done.8.values_ref), channel_id=1, source_target_pairs={{0,16},{1,9},{2,18},{3,11},{4,20},{5,13},{6,22},{7,15},{8,24},{9,1... | collective-permute-start | bytes 3145736 | tf_op jit(solution)/shard_map/ppermute | solution.py:38
  236.9 258.1 %reduce-scatter.4.cloned.1.call-start = ((), (), s32[]{:S(2)}) async-start(), calls=%async_computation.4 | async-start | bytes 6488064 | tf_op jit(solution)/shard_map/reduce_scatter | solution.py:437
  237.6 259.6 %reduce-scatter.8.cloned.1.call-start = ((), (), s32[]{:S(2)}) async-start(), calls=%async_computation.6 | async-start | bytes 6488064 | tf_op jit(solution)/shard_map/reduce_scatter | solution.py:437
  237.7 15.1 %collective-permute-start.12 = (bf16[256,2048]{1,0:T(8,128)(2,1)}, bf16[256,2048]{1,0:T(8,128)(2,1)S(1)}, u32[]{:S(2)}, u32[]{:S(2)}) collective-permute-start(bf16[256,2048]{1,0:T(8,128)(2,1)} %get-tuple-element.115), channel_id=1, source_target_pairs={{0,16},{1,9},{2,18},{3,11},{4,20},{5,13},{6,22},{7,15},{8,24},{9,1... | collective-permute-start | bytes 3145736 | tf_op jit(solution)/shard_map/ppermute | solution.py:38
  254.1 25.6 %copy-start.9 = (bf16[256,2048]{1,0:T(8,128)(2,1)S(1)}, bf16[256,2048]{1,0:T(8,128)(2,1)}, u32[]{:S(2)}) copy-start(bf16[256,2048]{1,0:T(8,128)(2,1)} %get-tuple-element.112) | copy-start | bytes 3145732
  254.1 25.6 %collective-permute-start.13 = (bf16[256,2048]{1,0:T(8,128)(2,1)}, bf16[256,2048]{1,0:T(8,128)(2,1)}, u32[]{:S(2)}, u32[]{:S(2)}) collective-permute-start(bf16[256,2048]{1,0:T(8,128)(2,1)} %add_convert_fusion), channel_id=1, source_target_pairs={{0,8},{1,17},{2,10},{3,19},{4,12},{5,21},{6,14},{7,23},{8,0},{9,25... | collective-permute-start | bytes 3145736 | tf_op jit(solution)/shard_map/ppermute | solution.py:38
  255.9 23.9 %collective-permute-start.11 = (bf16[256,2048]{1,0:T(8,128)(2,1)}, bf16[256,2048]{1,0:T(8,128)(2,1)}, u32[]{:S(2)}, u32[]{:S(2)}) collective-permute-start(bf16[256,2048]{1,0:T(8,128)(2,1)} %get-tuple-element.113), channel_id=1, source_target_pairs={{0,16},{1,9},{2,18},{3,11},{4,20},{5,13},{6,22},{7,15},{8,24},{9,1... | collective-permute-start | bytes 3145736 | tf_op jit(solution)/shard_map/ppermute | solution.py:38
  256.6 25.9 %copy-start.30 = (f32[8,1024]{1,0:T(8,128)}, f32[8,1024]{1,0:T(8,128)S(1)}, u32[]{:S(2)}) copy-start(f32[8,1024]{1,0:T(8,128)S(1)} %constant_dynamic-update-slice_fusion.4.lse_ref) | copy-start | bytes 98308
  286.8 24.6 %collective-permute-start.14 = (bf16[256,2048]{1,0:T(8,128)(2,1)}, bf16[256,2048]{1,0:T(8,128)(2,1)S(1)}, u32[]{:S(2)}, u32[]{:S(2)}) collective-permute-start(bf16[256,2048]{1,0:T(8,128)(2,1)} %get-tuple-element.175), channel_id=1, source_target_pairs={{0,8},{1,17},{2,10},{3,19},{4,12},{5,21},{6,14},{7,23},{8,0},{9,25... | collective-permute-start | bytes 3145736 | tf_op jit(solution)/shard_map/ppermute | solution.py:38
  287.0 24.5 %collective-permute-start.15 = (bf16[256,2048]{1,0:T(8,128)(2,1)}, bf16[256,2048]{1,0:T(8,128)(2,1)}, u32[]{:S(2)}, u32[]{:S(2)}) collective-permute-start(bf16[256,2048]{1,0:T(8,128)(2,1)} %get-tuple-element.175), channel_id=1, source_target_pairs={{0,16},{1,9},{2,18},{3,11},{4,20},{5,13},{6,22},{7,15},{8,24},{9,1... | collective-permute-start | bytes 3145736 | tf_op jit(solution)/shard_map/ppermute | solution.py:38
  311.5 20.3 %collective-permute-start.16 = (bf16[256,2048]{1,0:T(8,128)(2,1)S(1)}, bf16[256,2048]{1,0:T(8,128)(2,1)}, u32[]{:S(2)}, u32[]{:S(2)}) collective-permute-start(bf16[256,2048]{1,0:T(8,128)(2,1)S(1)} %collective-permute-done.14), channel_id=1, source_target_pairs={{0,16},{1,9},{2,18},{3,11},{4,20},{5,13},{6,22},{7,15},{8,24},{9,1... | collective-permute-start | bytes 3145736 | tf_op jit(solution)/shard_map/ppermute | solution.py:38
  359.6 9.0 %collective-permute-start.28 = (bf16[4,64,2048]{2,1,0:T(8,128)(2,1)}, bf16[4,64,2048]{2,1,0:T(8,128)(2,1)}, u32[]{:S(2)}, u32[]{:S(2)}) collective-permute-start(bf16[4,64,2048]{2,1,0:T(8,128)(2,1)} %dynamic-slice_bitcast_fusion), channel_id=1, source_target_pairs={{0,1},{1,0},{2,3},{3,2},{4,5},{5,4},{6,7},{7,6},{8,9},{9,8},{10,11... | collective-permute-start | bytes 3145736 | tf_op jit(solution)/shard_map/ppermute | solution.py:451
  368.1 21.9 %collective-permute-start.21 = (bf16[4,256,640]{1,2,0:T(8,128)(2,1)}, bf16[4,256,640]{1,2,0:T(8,128)(2,1)}, u32[]{:S(2)}, u32[]{:S(2)}) collective-permute-start(bf16[4,256,640]{1,2,0:T(8,128)(2,1)} %bitcast.111), channel_id=1, source_target_pairs={{0,1},{1,0},{2,3},{3,2},{4,5},{5,4},{6,7},{7,6},{8,9},{9,8},{10,11... | collective-permute-start | bytes 3932168 | tf_op jit(solution)/shard_map/ppermute | solution.py:451
  371.3 12.9 %collective-permute-start.29 = (bf16[64,2048]{1,0:T(8,128)(2,1)}, bf16[64,2048]{1,0:T(8,128)(2,1)}, u32[]{:S(2)}, u32[]{:S(2)}) collective-permute-start(bf16[64,2048]{1,0:T(8,128)(2,1)} %get-tuple-element.189), channel_id=1, source_target_pairs={{0,2},{1,3},{8,10},{9,11},{16,18},{17,19},{24,26},{25,27}} | collective-permute-start | bytes 786440 | tf_op jit(solution)/shard_map/ppermute | solution.py:460
  373.3 47.6 %collective-permute-start.17 = (bf16[512,2048]{1,0:T(8,128)(2,1)}, bf16[512,2048]{1,0:T(8,128)(2,1)}, u32[]{:S(2)}, u32[]{:S(2)}) collective-permute-start(bf16[512,2048]{1,0:T(8,128)(2,1)} %convolution_convert_fusion.9), channel_id=1, source_target_pairs={{0,16},{1,9},{2,18},{3,11},{4,20},{5,13},{6,22},{7,15},{8,24},{9,1... | collective-permute-start | bytes 6291464 | tf_op jit(solution)/shard_map/ppermute | solution.py:38
  376.1 17.9 %collective-permute-start.32 = (bf16[64,2048]{1,0:T(8,128)(2,1)S(1)}, bf16[64,2048]{1,0:T(8,128)(2,1)S(1)}, u32[]{:S(2)}, u32[]{:S(2)}) collective-permute-start(bf16[64,2048]{1,0:T(8,128)(2,1)S(1)} %get-tuple-element.190), channel_id=1, source_target_pairs={{6,4},{7,5},{14,12},{15,13},{22,20},{23,21},{30,28},{31,29}} | collective-permute-start | bytes 786440 | tf_op jit(solution)/shard_map/ppermute | solution.py:461
  385.3 17.0 %collective-permute-start.30 = (bf16[64,2048]{1,0:T(8,128)(2,1)S(1)}, bf16[64,2048]{1,0:T(8,128)(2,1)S(1)}, u32[]{:S(2)}, u32[]{:S(2)}) collective-permute-start(bf16[64,2048]{1,0:T(8,128)(2,1)S(1)} %fusion.46), channel_id=1, source_target_pairs={{0,2},{1,3},{2,4},{3,5},{8,10},{9,11},{10,12},{11,13},{16,18},{17,... | collective-permute-start | bytes 786440 | tf_op jit(solution)/shard_map/ppermute | solution.py:460
  392.1 24.2 %collective-permute-start.22 = (bf16[256,640]{0,1:T(8,128)(2,1)S(1)}, bf16[256,640]{0,1:T(8,128)(2,1)S(1)}, u32[]{:S(2)}, u32[]{:S(2)}) collective-permute-start(bf16[256,640]{0,1:T(8,128)(2,1)S(1)} %get-tuple-element.185), channel_id=1, source_target_pairs={{0,2},{1,3},{8,10},{9,11},{16,18},{17,19},{24,26},{25,27}} | collective-permute-start | bytes 983048 | tf_op jit(solution)/shard_map/ppermute | solution.py:460
  402.3 44.2 %slice-start.2 = ((s8[5767168]{0:T(1024)(128)(4,1)}), s8[4194304]{0:T(1024)(128)(4,1)S(1)}, s32[]{:S(2)}) async-start(s8[5767168]{0:T(1024)(128)(4,1)} %bitcast.115), calls=%async_computation.9 | async-start | bytes 8388608
  402.4 44.1 %slice-start.3 = ((s8[5767168]{0:T(1024)(128)(4,1)}), s8[1572864]{0:T(1024)(128)(4,1)S(1)}, s32[]{:S(2)}) async-start(s8[5767168]{0:T(1024)(128)(4,1)} %bitcast.115), calls=%async_computation.10 | async-start | bytes 3145728
  402.4 18.7 %collective-permute-start.33 = (bf16[64,2048]{1,0:T(8,128)(2,1)S(1)}, bf16[64,2048]{1,0:T(8,128)(2,1)S(1)}, u32[]{:S(2)}, u32[]{:S(2)}) collective-permute-start(bf16[64,2048]{1,0:T(8,128)(2,1)S(1)} %get-tuple-element.188), channel_id=1, source_target_pairs={{4,2},{5,3},{6,4},{7,5},{12,10},{13,11},{14,12},{15,13},{20,18},{2... | collective-permute-start | bytes 786440 | tf_op jit(solution)/shard_map/ppermute | solution.py:461
  405.0 41.5 %copy-start.6 = (bf16[1024,1408]{1,0:T(8,128)(2,1)S(1)}, bf16[1024,1408]{1,0:T(8,128)(2,1)}, u32[]{:S(2)}) copy-start(bf16[1024,1408]{1,0:T(8,128)(2,1)} %get-tuple-element.143) | copy-start | bytes 8650756
  405.1 17.4 %collective-permute-start.25 = (bf16[256,640]{0,1:T(8,128)(2,1)S(1)}, bf16[256,640]{0,1:T(8,128)(2,1)S(1)}, u32[]{:S(2)}, u32[]{:S(2)}) collective-permute-start(bf16[256,640]{0,1:T(8,128)(2,1)S(1)} %get-tuple-element.186), channel_id=1, source_target_pairs={{6,4},{7,5},{14,12},{15,13},{22,20},{23,21},{30,28},{31,29}} | collective-permute-start | bytes 983048 | tf_op jit(solution)/shard_map/ppermute | solution.py:461
  405.9 47.0 %collective-permute-start.31 = (bf16[64,2048]{1,0:T(8,128)(2,1)S(1)}, bf16[64,2048]{1,0:T(8,128)(2,1)S(1)}, u32[]{:S(2)}, u32[]{:S(2)}) collective-permute-start(bf16[64,2048]{1,0:T(8,128)(2,1)S(1)} %get-tuple-element.187), channel_id=1, source_target_pairs={{0,2},{1,3},{2,4},{3,5},{4,6},{5,7},{8,10},{9,11},{10,12},{11,13},... | collective-permute-start | bytes 786440 | tf_op jit(solution)/shard_map/ppermute | solution.py:460
  416.3 24.3 %collective-permute-start.23 = (bf16[256,640]{0,1:T(8,128)(2,1)S(1)}, bf16[256,640]{0,1:T(8,128)(2,1)S(1)}, u32[]{:S(2)}, u32[]{:S(2)}) collective-permute-start(bf16[256,640]{0,1:T(8,128)(2,1)S(1)} %fusion.40), channel_id=1, source_target_pairs={{0,2},{1,3},{2,4},{3,5},{8,10},{9,11},{10,12},{11,13},{16,18},{17,... | collective-permute-start | bytes 983048 | tf_op jit(solution)/shard_map/ppermute | solution.py:460
  421.0 34.4 %collective-permute-start.19 = (bf16[512,2048]{1,0:T(8,128)(2,1)S(1)}, bf16[512,2048]{1,0:T(8,128)(2,1)S(1)}, u32[]{:S(2)}, u32[]{:S(2)}) collective-permute-start(bf16[512,2048]{1,0:T(8,128)(2,1)S(1)} %copy-done.32), channel_id=1, source_target_pairs={{0,16},{1,9},{2,18},{3,11},{4,20},{5,13},{6,22},{7,15},{8,24},{9,1... | collective-permute-start | bytes 6291464 | tf_op jit(solution)/shard_map/ppermute | solution.py:38
  421.2 31.7 %collective-permute-start.34 = (bf16[64,2048]{1,0:T(8,128)(2,1)S(1)}, bf16[64,2048]{1,0:T(8,128)(2,1)S(1)}, u32[]{:S(2)}, u32[]{:S(2)}) collective-permute-start(bf16[64,2048]{1,0:T(8,128)(2,1)S(1)} %fusion.45), channel_id=1, source_target_pairs={{2,0},{3,1},{4,2},{5,3},{6,4},{7,5},{10,8},{11,9},{12,10},{13,11},... | collective-permute-start | bytes 786440 | tf_op jit(solution)/shard_map/ppermute | solution.py:461
  440.8 13.3 %collective-permute-start.26 = (bf16[256,640]{0,1:T(8,128)(2,1)S(1)}, bf16[256,640]{0,1:T(8,128)(2,1)S(1)}, u32[]{:S(2)}, u32[]{:S(2)}) collective-permute-start(bf16[256,640]{0,1:T(8,128)(2,1)S(1)} %get-tuple-element.184), channel_id=1, source_target_pairs={{4,2},{5,3},{6,4},{7,5},{12,10},{13,11},{14,12},{15,13},{20,18},{2... | collective-permute-start | bytes 983048 | tf_op jit(solution)/shard_map/ppermute | solution.py:461
  441.5 19.7 %collective-permute-start.24 = (bf16[256,640]{0,1:T(8,128)(2,1)S(1)}, bf16[256,640]{0,1:T(8,128)(2,1)S(1)}, u32[]{:S(2)}, u32[]{:S(2)}) collective-permute-start(bf16[256,640]{0,1:T(8,128)(2,1)S(1)} %get-tuple-element.183), channel_id=1, source_target_pairs={{0,2},{1,3},{2,4},{3,5},{4,6},{5,7},{8,10},{9,11},{10,12},{11,13},... | collective-permute-start | bytes 983048 | tf_op jit(solution)/shard_map/ppermute | solution.py:460
  452.9 17.5 %collective-permute-start.18 = (bf16[256,2048]{1,0:T(8,128)(2,1)}, bf16[256,2048]{1,0:T(8,128)(2,1)}, u32[]{:S(2)}, u32[]{:S(2)}) collective-permute-start(bf16[256,2048]{1,0:T(8,128)(2,1)} %slice.101), channel_id=1, source_target_pairs={{0,8},{1,17},{2,10},{3,19},{4,12},{5,21},{6,14},{7,23},{8,0},{9,25... | collective-permute-start | bytes 3145736 | tf_op jit(solution)/shard_map/ppermute | solution.py:38
  454.1 14.4 %collective-permute-start.27 = (bf16[256,640]{0,1:T(8,128)(2,1)S(1)}, bf16[256,640]{0,1:T(8,128)(2,1)S(1)}, u32[]{:S(2)}, u32[]{:S(2)}) collective-permute-start(bf16[256,640]{0,1:T(8,128)(2,1)S(1)} %fusion.39), channel_id=1, source_target_pairs={{2,0},{3,1},{4,2},{5,3},{6,4},{7,5},{10,8},{11,9},{12,10},{13,11},... | collective-permute-start | bytes 983048 | tf_op jit(solution)/shard_map/ppermute | solution.py:461
  459.4 19.8 %collective-permute-start.20 = (bf16[256,2048]{1,0:T(8,128)(2,1)}, bf16[256,2048]{1,0:T(8,128)(2,1)}, u32[]{:S(2)}, u32[]{:S(2)}) collective-permute-start(bf16[256,2048]{1,0:T(8,128)(2,1)} %slice.100), channel_id=1, source_target_pairs={{0,8},{1,17},{2,10},{3,19},{4,12},{5,21},{6,14},{7,23},{8,0},{9,25... | collective-permute-start | bytes 3145736 | tf_op jit(solution)/shard_map/ppermute | solution.py:38
  481.9 10.1 %all-to-all-start = ((f32[32,1,128]{2,1,0:T(1,128)}), f32[32,1,128]{2,1,0:T(1,128)S(1)}, u32[]{:S(2)}, u32[]{:S(2)}) async-start(f32[32,1,128]{2,1,0:T(1,128)} %bitcast.27), calls=%async_computation.3 | async-start | bytes 32768 | tf_op jit(solution)/shard_map/all_to_all | solution.py:604
  (32 other events, 313.0 us)
Sparse Core Ops, SparseCore 0:
  237.0 65.0 reduce-scatter.5
  304.4 63.2 reduce-scatter.3
  369.9 96.4 reduce-scatter.7
